TPU v7x, 32 devices: a whole 2x2x4 slice. The times are simulated.
32 devices in a mesh: ctx: 16 (over z, y, core), wt: 2 (over x).
Axes of the slice: x: 2, y: 2, z: 4, core: 2. Of those that a mesh axis runs over, the one named last changes fastest.
Arguments:
- block_in: bfloat16 [4, 4096, 512], P('wt', 'ctx'), may hold values from -6 to 6
- block_order: int32 [4, 32], P('wt'), may hold values from 0 to 31, as said below
- w_query: bfloat16 [512, 512], P('wt'), may hold values from -0.25 to 0.25
- b_query: bfloat16 [512], P('wt'), may hold values from -1.796875 to 1.796875
- w_key: bfloat16 [512, 512], P('wt'), may hold values from -0.25 to 0.25
- w_value: bfloat16 [512, 512], P('wt'), may hold values from -0.25 to 0.25
- b_value: bfloat16 [512], P('wt'), may hold values from -0.59765625 to 0.59765625
- w_out: bfloat16 [512, 512], P('wt'), may hold values from -1.5 to 1.5
- b_out: bfloat16 [512], P('wt'), may hold values from -1.796875 to 1.796875
- gain_one: bfloat16 [512], P('wt'), may hold values from 0.5 to 1.5
- shift_one: bfloat16 [512], P('wt'), may hold values from -1.796875 to 1.796875
- w_up: bfloat16 [512, 2048], P('wt'), may hold values from -0.25 to 0.25
- b_up: bfloat16 [2048], P('wt'), may hold values from -1.796875 to 1.796875
- w_down: bfloat16 [2048, 512], P('wt'), may hold values from -0.125 to 0.125
- b_down: bfloat16 [512], P('wt'), may hold values from -1.796875 to 1.796875
- gain_two: bfloat16 [512], P('wt'), may hold values from 0.5 to 1.5
- shift_two: bfloat16 [512], P('wt'), may hold values from -1.796875 to 1.796875
- cotangent: bfloat16 [4, 4096, 512], P('wt', 'ctx'), may hold values from -6 to 6
Outputs:
- block_out: bfloat16 [4, 4096, 512], P('wt', 'ctx')
- grad_in: bfloat16 [4, 4096, 512], P('wt', 'ctx')
- dw_query: float32 [512, 512], P('wt')
- db_query: float32 [512], P('wt')
- dw_key: float32 [512, 512], P('wt')
- dw_value: float32 [512, 512], P('wt')
- db_value: float32 [512], P('wt')
- dw_out: float32 [512, 512], P('wt')
- db_out: float32 [512], P('wt')
- dgain_one: float32 [512], P('wt')
- dshift_one: float32 [512], P('wt')
- dw_up: float32 [512, 2048], P('wt')
- db_up: float32 [2048], P('wt')
- dw_down: float32 [2048, 512], P('wt')
- db_down: float32 [512], P('wt')
- dgain_two: float32 [512], P('wt')
- dshift_two: float32 [512], P('wt')
Inputs may be any that keep to these rules, and one draw needn't show every extreme that they name: `block_order`: each row lists the 32 blocks of a sequence in stored order and is a permutation; entries 2 i and 2 i + 1 of a row sum to 31.
All inputs are finite; a program needn't handle non-finite values.
Results may differ from a plain program's by a relative error of at most 0.024.
Values may be sent and summed in bfloat16 or wider, within the bound.
A program may use at most 192 MiB of HBM per device.

v0:
```python
import functools
import math

import jax
import jax.numpy as jnp
from jax import lax
from jax.experimental import pallas as pl
from jax.experimental.pallas import tpu as pltpu
from jax.sharding import PartitionSpec as P

norm_eps = 1e-05

BLOCK = 128
HEADS_HERE = 4
LOG2E = 1.4426950408889634
FAR = -1e30
bf16, f32 = jnp.bfloat16, jnp.float32
NT = (((1,), (1,)), ((), ()))
TN = (((0,), (0,)), ((), ()))


def dot(a, b, dims=(((1,), (0,)), ((), ()))):
    return lax.dot_general(a, b, dims, preferred_element_type=f32)


def turned(v):
    return v.astype(f32).T.astype(bf16)


def head_slices():
    return [(slice(64 * h, 64 * h + 64), slice(128 * h, 128 * h + 128)) for h in range(HEADS_HERE)]


class Pairs:
    def __init__(self, nb, first):
        self.nb, self.first = nb, first

    def first_lo(self, n):
        return self.first(n) < self.nb // 2

    def lo(self, n):
        b = self.first(n)
        return jnp.where(b < self.nb // 2, b, self.nb - 1 - b)

    def ordered(self, n, v):
        a, b = v[:BLOCK], v[BLOCK:]
        first = self.first_lo(n)
        return jnp.where(first, a, b), jnp.where(first, b, a)


def project_chunk(pairs, r, x_ref, wkv_ref, wkvt_ref, bkv_ref, bkvt_ref, K, V, KT, VT):
    def piece(p, _):
        x = jnp.concatenate(pairs.ordered(r * 4 + p, x_ref[r, p]), axis=0)
        kv = dot(x, wkv_ref[...])
        k, v = kv[:, :256].astype(bf16), (kv[:, 256:] + bkv_ref[...]).astype(bf16)
        kvt = dot(wkvt_ref[...], x, NT)
        kt, vt = kvt[:256].astype(bf16), (kvt[256:] + bkvt_ref[...]).astype(bf16)
        at = pl.ds(pl.multiple_of(p * BLOCK, BLOCK), BLOCK)
        for u in range(2):
            rows = slice(u * BLOCK, (u + 1) * BLOCK)
            K[r, u, at, :] = k[rows]
            V[r, u, at, :] = v[rows]
            KT[r, u, :, at] = kt[:, rows]
            VT[r, u, :, at] = vt[:, rows]
        return 0
    lax.fori_loop(0, 4, piece, 0)


def project_queries(pairs, x_ref, wq_ref, bq_ref, qn, qt, qs):
    qs[...] = jnp.zeros_like(qs)

    def piece(p, _):
        x = jnp.concatenate(pairs.ordered(p, x_ref[0, p]), axis=0)
        q = (dot(x, wq_ref[...]) + bq_ref[...]) * (LOG2E / 8.0)
        for u in range(2):
            mine = q[u * BLOCK:(u + 1) * BLOCK]
            qn[p, u] = mine.astype(bf16)
            t = mine.T.astype(bf16)
            qt[p, u] = t
            for hs, cs in head_slices():
                qs[p, u, hs, cs] = t[hs]
        return 0
    lax.fori_loop(0, 4, piece, 0)


def by_pair(vt, p16):
    return jnp.concatenate([dot(vt[0:128], p16[:, 0:256]), dot(vt[128:256], p16[:, 256:512])], axis=1)


def unpair(a):
    return jnp.concatenate([a[64 * (h % 2):64 * (h % 2) + 64, 128 * h:128 * h + 128] for h in range(HEADS_HERE)], axis=0)


def fwd_step(pairs, r, i, own, K, VT, qs, m_s, l_s, acc, d_s, sb, pb):
    col = lambda v: jnp.max(v, axis=0, keepdims=True)
    tot = lambda v: jnp.sum(v, axis=0, keepdims=True)
    lo_i = pairs.lo(i)
    pick = [lo_i > pairs.lo(r * 4 + j) for j in range(4)]
    sa = dot(K[r, 0], qs[i, 1])
    for j in range(4):
        u = jnp.where(pick[j], 0, 1)
        s = dot(K[r, u, j * BLOCK:(j + 1) * BLOCK, :], qs[i, u])
        if own:
            s = jnp.where(d_s[...] <= jnp.where(i == j, 0, 2 * BLOCK), s, FAR)
        sb[j] = s
    tops = [col(sb[j]) for j in range(4)]
    m_hi, m_lo = col(sa), None
    for j in range(4):
        m_hi = jnp.maximum(m_hi, jnp.where(pick[j], FAR, tops[j]))
        t = jnp.where(pick[j], tops[j], FAR)
        m_lo = t if m_lo is None else jnp.maximum(m_lo, t)
    if own:
        rows = pl.ds(pl.multiple_of(i * BLOCK, BLOCK), BLOCK)
        sd = jnp.where(d_s[...] <= 0, dot(K[r, 0, rows, :], qs[i, 0]), FAR)
        m_lo = jnp.maximum(m_lo, col(sd))
    else:
        old_hi, old_lo = m_s[i, 1], m_s[i, 0]
        m_hi, m_lo = jnp.maximum(m_hi, old_hi), jnp.maximum(m_lo, old_lo)
    pa = jnp.exp2(sa - m_hi)
    l_hi, l_lo = tot(pa), jnp.zeros((1, 512), f32)
    for j in range(4):
        p = jnp.exp2(sb[j] - jnp.where(pick[j], m_lo, m_hi))
        t = tot(p)
        l_hi = l_hi + jnp.where(pick[j], 0.0, t)
        l_lo = l_lo + jnp.where(pick[j], t, 0.0)
        low = p.astype(bf16)
        rows = slice(j * BLOCK, (j + 1) * BLOCK)
        zero = jnp.zeros_like(low)
        pb[0, rows, :] = jnp.where(pick[j], low, zero)
        pb[1, rows, :] = jnp.where(pick[j], zero, low)
    o_hi = by_pair(VT[r, 0], pa.astype(bf16)) + by_pair(VT[r, 1], pb[1])
    o_lo = by_pair(VT[r, 0], pb[0])
    if own:
        p = jnp.exp2(sd - m_lo)
        l_lo = l_lo + tot(p)
        at = pl.ds(pl.multiple_of(i * BLOCK, BLOCK), BLOCK)
        o_lo = o_lo + by_pair(VT[r, 0, :, at], p.astype(bf16))
        l_s[i, 1], l_s[i, 0] = l_hi, l_lo
        acc[i, 1], acc[i, 0] = o_hi, o_lo
    else:
        f_hi, f_lo = jnp.exp2(old_hi - m_hi), jnp.exp2(old_lo - m_lo)
        l_s[i, 1] = l_s[i, 1] * f_hi + l_hi
        l_s[i, 0] = l_s[i, 0] * f_lo + l_lo
        acc[i, 1] = acc[i, 1] * f_hi + o_hi
        acc[i, 0] = acc[i, 0] * f_lo + o_lo
    m_s[i, 1], m_s[i, 0] = m_hi, m_lo


def fwd_finish(pairs, m_s, l_s, acc, lse, ot, o_ref):
    def pair(i, _):
        first = pairs.first_lo(i)
        out = []
        for u in range(2):
            l = l_s[i, u]
            lse[i, u] = m_s[i, u] + jnp.log2(l)
            t = unpair(acc[i, u] * (1.0 / l))
            ot[i, u] = t
            out.append(t.T.astype(bf16))
        o_ref[i, 0:BLOCK, :] = jnp.where(first, out[0], out[1])
        o_ref[i, BLOCK:2 * BLOCK, :] = jnp.where(first, out[1], out[0])
        return 0
    lax.fori_loop(0, 4, pair, 0)


def diagonal(d_s):
    d_s[...] = lax.broadcasted_iota(jnp.int32, d_s.shape, 0) - (lax.broadcasted_iota(jnp.int32, d_s.shape, 1) & (BLOCK - 1))


def fwd_local(nz, blk_ref, x_ref, wqkv_ref, bq_ref, bkv_ref, bkvt_ref, o_ref, ot, lse, K, V, KT, qn, qt, VT, qs, m_s, l_s, acc, d_s, sb, pb, wkvt):
    pairs = Pairs(nz * 8, lambda n: blk_ref[2 * n])
    diagonal(d_s)
    wkvt[...] = turned(wqkv_ref[:, 256:])
    project_queries(pairs, x_ref, wqkv_ref.at[:, 0:256], bq_ref, qn, qt, qs)
    for r in range(nz):
        project_chunk(pairs, r, x_ref, wqkv_ref.at[:, 256:768], wkvt, bkv_ref, bkvt_ref, K, V, KT, VT)
        def step(i, _):
            fwd_step(pairs, r, i, r == 0, K, VT, qs, m_s, l_s, acc, d_s, sb, pb)
            return 0
        lax.fori_loop(0, 4, step, 0)
    fwd_finish(pairs, m_s, l_s, acc, lse, ot, o_ref)


def fwd_outs(nz):
    sds = jax.ShapeDtypeStruct
    kv = sds((nz, 2, 512, 256), bf16)
    return (sds((4, 256, 256), bf16), sds((4, 2, 256, 128), f32), sds((4, 2, 1, 512), f32), kv, kv, sds((nz, 2, 256, 512), bf16),
            sds((4, 2, 128, 256), bf16), sds((4, 2, 256, 128), bf16))


def fwd_scratch(nz):
    M = pltpu.VMEM
    return [M((nz, 2, 256, 512), bf16), M((4, 2, 256, 512), bf16), M((4, 2, 1, 512), f32), M((4, 2, 1, 512), f32), M((4, 2, 128, 512), f32),
            M((128, 512), jnp.int32), M((4, 128, 512), f32), M((2, 512, 512), bf16), M((512, 512), bf16)]


def attn_fwd(nz, blk, x, wqkv, bq, bkv):
    V = pl.BlockSpec(memory_space=pltpu.VMEM)
    return pl.pallas_call(
        functools.partial(fwd_local, nz), out_shape=fwd_outs(nz),
        in_specs=[pl.BlockSpec(memory_space=pltpu.SMEM)] + [V] * 5, out_specs=(V,) * 8, scratch_shapes=fwd_scratch(nz),
        compiler_params=pltpu.CompilerParams(vmem_limit_bytes=58 << 20), name="attn_fwd")(blk, x, wqkv, bq, bkv, bkv.reshape(256, 1))


def bwd_queries(pairs, do_ref, ot, qn, qt, qs, dos, qns, dons, dl):
    def piece(i, _):
        for u, do in enumerate(pairs.ordered(i, do_ref[i])):
            dot_t = do.astype(f32).T
            prod = dot_t * ot[i, u]
            low = dot_t.astype(bf16)
            q, t = qn[i, u], qt[i, u]
            for hs, cs in head_slices():
                qs[i, u, hs, cs] = t[hs]
                dos[i, u, hs, cs] = low[hs]
                qns[i, u, cs, hs] = q[:, hs]
                dons[i, u, cs, hs] = do[:, hs]
                dl[i, u, :, cs] = jnp.sum(prod[hs], axis=0, keepdims=True)
        return 0
    lax.fori_loop(0, 4, piece, 0)


def bwd_step(pairs, r, i, own, first, K, V, KT, qs, dos, qns, dons, lse, dl, dk, dv, dq, d_s, gb, js=(0, 1, 2, 3)):
    lo_i = pairs.lo(i)
    pick = {j: lo_i > pairs.lo(r * 4 + j) for j in js}
    part = slice(js[0] * BLOCK, js[-1] * BLOCK + BLOCK)

    def pieces(k, v, u, mask):
        s = dot(k, qs[i, u]) - lse[i, u]
        if mask is not None:
            s = jnp.where(d_s[...] <= mask, s, FAR)
        p = jnp.exp2(s)
        g = p * (dot(v, dos[i, u]) - dl[i, u])
        return p.astype(bf16), g.astype(bf16)

    p, g = pieces(K[r, 0, part, :], V[r, 0, part, :], 1, None)
    dv[0, part, :] += dot(p, dons[i, 1])
    dk[0, part, :] += dot(g, qns[i, 1])
    q_hi = by_pair(KT[r, 0, :, part], g)
    for j in js:
        u = jnp.where(pick[j], 0, 1)
        rows = slice(j * BLOCK, (j + 1) * BLOCK)
        p, g = pieces(K[r, u, rows, :], V[r, u, rows, :], u, jnp.where(i == j, 0, 2 * BLOCK) if own else None)
        gv, gk = dot(p, dons[i, u]), dot(g, qns[i, u])
        dv[0, rows, :] += jnp.where(pick[j], gv, 0.0)
        dv[1, rows, :] += jnp.where(pick[j], 0.0, gv)
        dk[0, rows, :] += jnp.where(pick[j], gk, 0.0)
        dk[1, rows, :] += jnp.where(pick[j], 0.0, gk)
        zero = jnp.zeros_like(g)
        gb[0, rows, :] = jnp.where(pick[j], g, zero)
        gb[1, rows, :] = jnp.where(pick[j], zero, g)
    q_hi = q_hi + by_pair(KT[r, 1, :, part], gb[1, part, :])
    q_lo = by_pair(KT[r, 0, :, part], gb[0, part, :])
    if own:
        rows = pl.ds(pl.multiple_of(i * BLOCK, BLOCK), BLOCK)
        p, g = pieces(K[r, 0, rows, :], V[r, 0, rows, :], 0, 0)
        dv[0, rows, :] += dot(p, dons[i, 0])
        dk[0, rows, :] += dot(g, qns[i, 0])
        q_lo = q_lo + by_pair(KT[r, 0, :, rows], g)
    if first:
        dq[i, 1], dq[i, 0] = q_hi, q_lo
    else:
        dq[i, 1] += q_hi
        dq[i, 0] += q_lo


def bwd_chunk_weights(pairs, r, x_ref, dk, dv, dw, db, gp, js=(0, 1, 2, 3)):
    total = jnp.zeros((1, 256), f32)
    for p in js:
        at = slice(p * BLOCK, (p + 1) * BLOCK)
        g = [jnp.concatenate([(dk[u, at, :] * (1.0 / LOG2E)).astype(bf16), dv[u, at, :].astype(bf16)], axis=1) for u in range(2)]
        total = total + jnp.sum(g[0][:, 256:].astype(f32), axis=0, keepdims=True) + jnp.sum(g[1][:, 256:].astype(f32), axis=0, keepdims=True)
        first = pairs.first_lo(r * 4 + p)
        gp[p * 256:p * 256 + BLOCK, :] = jnp.where(first, g[0], g[1])
        gp[p * 256 + BLOCK:p * 256 + 256, :] = jnp.where(first, g[1], g[0])
    db[1:2, :] += total
    n = len(js)
    dw[:, 256:768] += dot(x_ref[r, js[0]:js[0] + n].reshape(n * 256, 512), gp[js[0] * 256:(js[0] + n) * 256, :], TN)


def bwd_chunk_rows(r, last, wqkv_ref, dxq, dx, gp, js=(1, 3, 0, 2)):
    for p in js:
        rows = slice(p * 256, p * 256 + 256)
        d = dot(gp[rows, :], wqkv_ref[:, 256:768], NT)
        if last:
            d = d + dxq[p]
        dx[r, rows, :] = d.astype(bf16)


def bwd_query_out(pairs, x_ref, wqkv_ref, dq, dxq, dw, db):
    def piece(i, _):
        t = [(unpair(dq[i, u]) * 0.125).T.astype(bf16) for u in range(2)]
        first = pairs.first_lo(i)
        g = jnp.concatenate([jnp.where(first, t[0], t[1]), jnp.where(first, t[1], t[0])], axis=0)
        dxq[i] = dot(g, wqkv_ref[:, 0:256], NT)
        dw[:, 0:256] += dot(x_ref[0, i], g, TN)
        db[0:1, :] += jnp.sum(g.astype(f32), axis=0, keepdims=True)
        return 0
    lax.fori_loop(0, 4, piece, 0)


def weight_rows(dw, gq):
    for k in range(2):
        for m in range(3):
            gq[k, m * 256:m * 256 + 256, :] = dw[k * 256:k * 256 + 256, m * 256:m * 256 + 256].astype(bf16)


def bwd_local(nz, blk_ref, x_ref, wqkv_ref, K, V, KT, qn, qt, ot, lse, do_ref, dx, gq, db, qs, dos, qns, dons, dl, dk, dv, dq, d_s, gb, dxq, dw, gp):
    pairs = Pairs(nz * 8, lambda n: blk_ref[2 * n])
    diagonal(d_s)
    dw[...] = jnp.zeros_like(dw)
    db[...] = jnp.zeros_like(db)
    for s in (qs, dos, qns, dons):
        s[...] = jnp.zeros_like(s)
    bwd_queries(pairs, do_ref, ot, qn, qt, qs, dos, qns, dons, dl)
    for r in list(range(1, nz)) + [0]:
        dk[...] = jnp.zeros_like(dk)
        dv[...] = jnp.zeros_like(dv)
        def step(i, _):
            bwd_step(pairs, r, i, r == 0, r == 1, K, V, KT, qs, dos, qns, dons, lse, dl, dk, dv, dq, d_s, gb)
            return 0
        lax.fori_loop(0, 4, step, 0)
        if r == 0:
            bwd_query_out(pairs, x_ref, wqkv_ref, dq, dxq, dw, db)
        bwd_chunk_weights(pairs, r, x_ref, dk, dv, dw, db, gp)
        bwd_chunk_rows(r, r == 0, wqkv_ref, dxq, dx, gp)
    weight_rows(dw, gq)


def bwd_scratch():
    M = pltpu.VMEM
    return [M((4, 2, 256, 512), bf16), M((4, 2, 256, 512), bf16), M((4, 2, 512, 256), bf16), M((4, 2, 512, 256), bf16), M((4, 2, 1, 512), f32),
            M((2, 512, 256), f32), M((2, 512, 256), f32), M((4, 2, 128, 512), f32), M((128, 512), jnp.int32), M((2, 512, 512), bf16),
            M((4, 256, 512), f32), M((512, 768), f32)]


def attn_bwd(nz, blk, x, wqkv, K, V, KT, qn, qt, ot, lse, do):
    S = pl.BlockSpec(memory_space=pltpu.VMEM)
    sds = jax.ShapeDtypeStruct
    return pl.pallas_call(
        functools.partial(bwd_local, nz), out_shape=(sds((nz, 1024, 512), bf16), sds((2, 768, 256), bf16), sds((8, 256), f32)),
        in_specs=[pl.BlockSpec(memory_space=pltpu.SMEM)] + [S] * 10, out_specs=(S,) * 3, scratch_shapes=bwd_scratch() + [pltpu.VMEM((1024, 512), bf16)],
        compiler_params=pltpu.CompilerParams(vmem_limit_bytes=58 << 20), name="attn_bwd")(blk, x, wqkv, K, V, KT, qn, qt, ot, lse, do)


def dense_kernel(x_ref, cot_ref, att_ref, wo_ref, wu_ref, wd_ref, sm_ref,
                 out_ref, dsm_ref, do_ref, gw_ref, gv_ref, act_s, gp_s, norm_s, dpre_s):
    ff = wu_ref.shape[1]
    chunk = 512
    x = x_ref[...].astype(f32)
    vec = lambda i: jnp.concatenate([sm_ref[0, i:i + 1, :], sm_ref[1, i:i + 1, :]], axis=1)
    b_out, g1, s1, b_down, g2, s2 = (vec(i) for i in range(2, 8))
    mean = lambda v: jnp.mean(v, axis=-1, keepdims=True)
    col = lambda v: jnp.sum(v, axis=0, keepdims=True)
    mix = x + dot(att_ref[...], wo_ref[...]) + b_out
    cen = mix - mean(mix)
    r1 = lax.rsqrt(mean(cen * cen) + norm_eps)
    n1 = cen * r1
    normed = n1 * g1 + s1
    nlow = normed.astype(bf16)
    norm_s[...] = nlow
    ffn = None
    for f in range(0, ff, chunk):
        fs = slice(f, f + chunk)
        at = 8 + f % (ff // 2) // 256
        b_up = jnp.concatenate([sm_ref[2 * f // ff, at + k:at + k + 1, :] for k in range(chunk // 256)], axis=1)
        pre = dot(nlow, wu_ref[:, fs]) + b_up
        c0 = math.sqrt(2.0 / math.pi)
        sq = pre * pre
        th = jnp.tanh(c0 * pre * (1.0 + 0.044715 * sq))
        half = 0.5 * (1.0 + th)
        act = (pre * half).astype(bf16)
        act_s[:, fs] = act
        gp_s[:, fs] = half + 0.5 * pre * (1.0 - th * th) * (c0 * (1.0 + 3 * 0.044715 * sq))
        part = dot(act, wd_ref[fs, :])
        ffn = part if ffn is None else ffn + part
    summed = ffn + b_down + normed + x
    cen = summed - mean(summed)
    r2 = lax.rsqrt(mean(cen * cen) + norm_eps)
    n2 = cen * r2
    out_ref[...] = (n2 * g2 + s2).astype(bf16)
    up = cot_ref[...].astype(f32)
    gv_ref[4:5, :] = col(up * n2)
    gv_ref[5:6, :] = col(up)
    dn = up * g2
    dsum = r2 * (dn - mean(dn) - n2 * mean(dn * n2))
    dffn = dsum.astype(bf16)
    gv_ref[3:4, :] = col(dffn.astype(f32))
    dnorm = dsum
    half_rows = wo_ref.shape[0] // 2
    half_ff = ff // 2
    def put(g, at, rows):
        gw_ref[0, at:at + rows, :] = g[:rows].astype(bf16)
        gw_ref[1, at:at + rows, :] = g[rows:].astype(bf16)
    for f in range(0, ff, chunk):
        fs = slice(f, f + chunk)
        dact = dot(dffn, wd_ref[fs, :], NT)
        dpre = (dact * gp_s[:, fs]).astype(bf16)
        gv_ref[8 + f // chunk:9 + f // chunk, :] = col(dpre.astype(f32))
        dnorm = dnorm + dot(dpre, wu_ref[:, fs], NT)
        put(dot(norm_s[...], dpre, TN), half_rows + (f // chunk) * half_rows, half_rows)
        gd = dot(act_s[:, fs], dffn, TN).astype(bf16)
        base = half_rows * (1 + ff // chunk)
        which, off = f // half_ff, f % half_ff
        gw_ref[which, base + off:base + off + chunk, :] = gd
    gv_ref[1:2, :] = col(dnorm * n1)
    gv_ref[2:3, :] = col(dnorm)
    dn = dnorm * g1
    dmix = r1 * (dn - mean(dn) - n1 * mean(dn * n1))
    dsm_ref[...] = dsum + dmix
    dbr = dmix.astype(bf16)
    gv_ref[0:1, :] = col(dbr.astype(f32))
    do_ref[...] = dot(dbr, wo_ref[...], NT).astype(bf16)
    put(dot(att_ref[...], dbr, TN), 0, half_rows)


def dense(x, cot, att, wo, wu, wd, sm):
    V = pl.BlockSpec(memory_space=pltpu.VMEM)
    tok, dim = x.shape
    ff = wu.shape[1]
    rows = (2 * dim * ff + dim * dim) // 2 // dim
    return pl.pallas_call(
        dense_kernel,
        out_shape=(jax.ShapeDtypeStruct((tok, dim), bf16), jax.ShapeDtypeStruct((tok, dim), f32),
                   jax.ShapeDtypeStruct((tok, dim), bf16), jax.ShapeDtypeStruct((2, rows, dim), bf16),
                   jax.ShapeDtypeStruct((16, dim), f32)),
        in_specs=[V] * 7, out_specs=(V,) * 5,
        scratch_shapes=[pltpu.VMEM((tok, ff), bf16), pltpu.VMEM((tok, ff), f32), pltpu.VMEM((tok, dim), bf16),
                        pltpu.VMEM((8, 128), f32)],
        compiler_params=pltpu.CompilerParams(vmem_limit_bytes=56 << 20),
        name="dense")(x, cot, att, wo, wu, wd, sm)


MESH = pl.DeviceIdType.MESH


def places(nz):
    me, wi = lax.axis_index("ctx"), lax.axis_index("wt")
    z, y, c = me // 4, lax.rem(me // 2, 2), lax.rem(me, 2)
    low = lax.rem(me, 4)
    at = lambda zz, ll: (zz * 4 + ll, wi)
    to = dict(up=at(lax.rem(z + 1, nz), low), down=at(lax.rem(z + nz - 1, nz), low), core=at(z, low + 1 - 2 * c), y=at(z, low + 2 - 4 * y),
              x=(me, 1 - wi))
    return me, wi, z, y, c, low, to


def meet(targets):
    bar = pltpu.get_barrier_semaphore()
    for t in targets:
        pl.semaphore_signal(bar, inc=1, device_id=t, device_id_type=MESH)
    pl.semaphore_wait(bar, len(targets))


class Wires:
    def __init__(self, send, recv):
        self.send, self.recv, self.n, self.live = send, recv, 0, []

    def make(self, src, dst, to):
        cp = pltpu.make_async_remote_copy(src, dst, self.send.at[self.n], self.recv.at[self.n], device_id=to, device_id_type=MESH)
        self.n += 1
        self.live.append(cp)
        return cp

    def go(self, src, dst, to):
        cp = self.make(src, dst, to)
        cp.start()
        return cp

    def drain(self):
        for cp in self.live:
            cp.wait_send()


def rows_of(start, size, mult=16):
    return pl.ds(pl.multiple_of(start, mult), size)


def gather_kernel(nz, with_w, *refs):
    if with_w:
        (x_ref, wq_ref, wk_ref, wv_ref, wo_ref, wu_ref, wd_ref, sm_ref,
         xall, wqkv, wo, wu, wd, sm, send, recv, lsem) = refs
    else:
        x_ref, xall, send, recv, lsem = refs
    me, wi, z, y, c, low, to = places(nz)
    rows = x_ref.shape[1]
    local = []

    def copy(src, dst):
        cp = pltpu.make_async_copy(src, dst, lsem.at[len(local)])
        cp.start()
        local.append(cp)

    copy(x_ref.at[y], xall.at[0, 0])
    if with_w:
        R, half = wq_ref.shape[0], wq_ref.shape[1] // 2
        for i, w in enumerate((wq_ref, wk_ref, wv_ref)):
            copy(w.at[:, rows_of(c * half, half, 128)], wqkv.at[rows_of(wi * R, R), pl.ds(i * half, half)])
        for w, full in ((wo_ref, wo), (wu_ref, wu), (wd_ref, wd)):
            n = w.shape[0]
            copy(w, full.at[rows_of(wi * n, n)])
        copy(sm_ref, sm.at[wi])
    near = [to["up"], to["down"], to["core"], to["y"]] + ([to["x"]] if with_w else [])
    meet(near)
    wires = Wires(send, recv)
    yx = wires.go(x_ref.at[1 - y], xall.at[0, 2], to["y"])
    ring = {(1, 0): wires.go(x_ref.at[y], xall.at[1, 0], to["up"])}
    core = {(0, 0): wires.go(x_ref.at[y], xall.at[0, 1], to["core"])}
    if with_w:
        xs = []
        for i, w in enumerate((wq_ref, wk_ref, wv_ref)):
            xs.append(wires.go(w.at[:, rows_of(c * half, half, 128)], wqkv.at[rows_of(wi * R, R), pl.ds(i * half, half)], to["x"]))
        xs.append(wires.go(sm_ref, sm.at[wi], to["x"]))
        big = []
        for w, full in ((wo_ref, wo), (wu_ref, wu), (wd_ref, wd)):
            n = w.shape[0]
            h = n // 2
            cp = wires.go(w.at[rows_of(c * h, h)], full.at[rows_of(wi * n + c * h, h)], to["x"])
            big.append((cp, full, rows_of((1 - wi) * n + c * h, h)))
    yx.wait_recv()
    ring[1, 1] = wires.go(xall.at[0, 2], xall.at[1, 2], to["up"])
    core[0, 1] = wires.go(xall.at[0, 2], xall.at[0, 3], to["core"])
    shared = []
    for r in range(1, nz):
        for s in range(2):
            ring[r, s].wait_recv()
            if r < nz - 1:
                ring[r + 1, s] = wires.go(xall.at[r, 2 * s], xall.at[r + 1, 2 * s], to["up"])
            core[r, s] = wires.go(xall.at[r, 2 * s], xall.at[r, 2 * s + 1], to["core"])
        if with_w and r - 1 < len(big):
            cp, full, where = big[r - 1]
            cp.wait_recv()
            shared.append(wires.go(full.at[where], full.at[where], to["core"]))
    if with_w:
        for cp, full, where in big[nz - 1:]:
            cp.wait_recv()
            shared.append(wires.go(full.at[where], full.at[where], to["core"]))
        for cp in xs + shared:
            cp.wait_recv()
    for cp in core.values():
        cp.wait_recv()
    wires.drain()
    for cp in local:
        cp.wait()


def gather_all(nz, x, weights=None, small=None):
    A = pl.BlockSpec(memory_space=pl.ANY)
    sds = jax.ShapeDtypeStruct
    rows, dim = x.shape[1:]
    outs = [sds((nz, 4, rows, dim), bf16)]
    ins = [x]
    ncopy = 1 + 2 * (nz - 1) + 2 * nz
    if weights is not None:
        wq, wk, wv, wo, wu, wd = weights
        ins += list(weights) + [small]
        outs += [sds((dim, 3 * dim // 2), bf16)] + [sds((2 * w.shape[0], w.shape[1]), bf16) for w in (wo, wu, wd)] + [sds((2,) + small.shape, bf16)]
        ncopy += 10
    return pl.pallas_call(
        functools.partial(gather_kernel, nz, weights is not None),
        out_shape=tuple(outs), in_specs=[A] * len(ins), out_specs=(A,) * len(outs),
        scratch_shapes=[pltpu.SemaphoreType.DMA((ncopy,)), pltpu.SemaphoreType.DMA((ncopy,)), pltpu.SemaphoreType.DMA((8,))],
        compiler_params=pltpu.CompilerParams(collective_id=1, has_side_effects=True, vmem_limit_bytes=16 << 20),
        name="gather_all")(*ins)


def add_into(dst, parts, rows, step=64):
    def body(i, _):
        r = rows_of(i * step, step)
        total = parts[0](r)[...].astype(f32)
        for p in parts[1:]:
            total = total + p(r)[...].astype(f32)
        d = dst(r)
        d[...] = total.astype(bf16)
        return 0
    lax.fori_loop(0, rows // step, body, 0)


def offset(ref, lead, start):
    def view(r):
        at = pl.ds(pl.multiple_of(start + r.start, 16), r.size)
        return ref.at[lead + (at,)]
    return view


def chip_pairs(nz, order_ref):
    me = lax.axis_index("ctx")
    z, y, c = me // 4, lax.rem(me // 2, 2), lax.rem(me, 2)

    def first(n):
        r, p = n // 4, n % 4
        a, b = p // 2, p % 2
        yy, cc = y + a - 2 * y * a, c + b - 2 * c * b
        return order_ref[y, 2 * (lax.rem(z - r + nz, nz) * 4 + yy * 2 + cc)]
    return Pairs(nz * 8, first)


def front_kernel(nz, order_ref, bqr, bvr, bor, g1r, s1r, bdr, g2r, s2r, bur, x_ref, wq_ref, wk_ref, wv_ref, wo_ref, wu_ref, wd_ref,
                 att, wo, wu, wd, sm, xall, wqkv, ot_o, lse_o, K_o, V_o, KT_o, qn_o, qt_o,
                 xs, ws, sms, wos, wus, wds, K, V, KT, VT, qn, qt, qs, m_s, l_s, acc, d_s, sb, pb, wkvt, bkvt, ot, lse, o_s, send, recv, lsem):
    me, wi, z, y, c, low, to = places(nz)
    to["yc"] = (z * 4 + 3 - low, wi)
    half, R = 256, wq_ref.shape[0]
    local = []

    def copy(src, dst):
        cp = pltpu.make_async_copy(src, dst, lsem.at[len(local)])
        cp.start()
        local.append(cp)
        return cp

    own_x = copy(x_ref.at[y], xs.at[0, 0])
    own_w = [copy(w.at[:, rows_of(c * half, half, 128)], ws.at[rows_of(wi * R, R), pl.ds(i * half, half)]) for i, w in enumerate((wq_ref, wk_ref, wv_ref))]
    for i, v in enumerate((bqr, bvr, bor, g1r, s1r, bdr, g2r, s2r)):
        sms[wi, i:i + 1, :] = v[...].astype(f32).reshape(1, half)
    up_b = bur[...].astype(f32).reshape(1, 1024)
    for i in range(4):
        sms[wi, 8 + i:9 + i, :] = up_b[:, i * half:(i + 1) * half]
    sms[wi, 12:16, :] = jnp.zeros((4, half), f32)
    meet([to[k] for k in ("up", "down", "core", "y", "yc", "x")])
    w = Wires(send, recv)
    yx = w.go(x_ref.at[1 - y], xs.at[0, 2], to["y"])
    ring, core = {}, {}
    ring[1, 0] = w.go(x_ref.at[y], xs.at[1, 0], to["up"])
    core[0, 0] = w.go(x_ref.at[y], xs.at[0, 1], to["core"])
    wx = []
    for i, m in enumerate((wq_ref, wk_ref, wv_ref)):
        wx.append(w.go(m.at[:, rows_of(c * half, half, 128)], ws.at[rows_of(wi * R, R), pl.ds(i * half, half)], to["x"]))
    wx.append(w.go(sms.at[wi], sms.at[wi], to["x"]))
    big = []
    for m, full in ((wo_ref, wos), (wu_ref, wus), (wd_ref, wds)):
        n = m.shape[0]
        h = n // 2
        copy(m, full.at[rows_of(wi * n, n)])
        big.append((m.at[rows_of(c * h, h)], full.at[rows_of(wi * n + c * h, h)], full, rows_of((1 - wi) * n + c * h, h)))

    pairs = chip_pairs(nz, order_ref)
    diagonal(d_s)
    yx.wait_recv()
    ring[1, 1] = w.go(xs.at[0, 2], xs.at[1, 2], to["up"])
    core[0, 1] = w.go(xs.at[0, 2], xs.at[0, 3], to["core"])

    def pump(r, s):
        ring[r, s].wait_recv()
        if r < nz - 1:
            ring[r + 1, s] = w.go(xs.at[r, 2 * s], xs.at[r + 1, 2 * s], to["up"])
        core[r, s] = w.go(xs.at[r, 2 * s], xs.at[r, 2 * s + 1], to["core"])

    shared = []

    def share(k):
        cp, full, where = sent[k]
        cp.wait_recv()
        shared.append(w.go(full.at[where], full.at[where], to["core"]))

    pump(1, 0)
    for cp in own_w:
        cp.wait()
    for cp in wx:
        cp.wait_recv()
    sent = [(w.go(src, dst, to["x"]), full, where) for src, dst, full, where in big]
    copy(sms, sm)
    copy(ws, wqkv)
    wkvt[...] = turned(ws[:, 256:])
    bv = sms[c, 1:2, :]
    bkvt[...] = jnp.broadcast_to(bv, (8, half)).T[:, 0:1]
    own_x.wait()
    for s in range(2):
        core[0, s].wait_recv()
    project_queries(pairs, xs, ws.at[:, 0:256], sms.at[c, 0:1], qn, qt, qs)
    copy(qn, qn_o)
    copy(qt, qt_o)

    def chunk(r):
        project_chunk(pairs, r, xs, ws.at[:, 256:768], wkvt, sms.at[c, 1:2], bkvt, K, V, KT, VT)
        for a, b in ((xs, xall), (K, K_o), (V, V_o), (KT, KT_o)):
            copy(a.at[r], b.at[r])

    def attend(r, start, stop):
        def step(i, _):
            fwd_step(pairs, r, i, r == 0, K, VT, qs, m_s, l_s, acc, d_s, sb, pb)
            return 0
        lax.fori_loop(start, stop, step, 0)

    chunk(0)
    pump(1, 1)
    attend(0, 0, 2)
    attend(0, 2, 4)
    for r in range(1, nz):
        if r + 1 < nz:
            pump(r + 1, 0)
        for s in range(2):
            core[r, s].wait_recv()
        chunk(r)
        attend(r, 0, 2)
        if r + 1 < nz:
            pump(r + 1, 1)
            share(r - 1)
        attend(r, 2, 4)
    fwd_finish(pairs, m_s, l_s, acc, lse, ot, o_s)
    cols = pl.ds(pl.multiple_of(c * half, half), half)
    outs = [w.go(o_s.at[p], att.at[y, :, cols], to[k]) for p, k in ((1, "core"), (2, "y"), (3, "yc"))]
    copy(o_s.at[0], att.at[y, :, cols])
    copy(ot, ot_o)
    copy(lse, lse_o)
    share(2)
    for k, (a, b) in enumerate(((wos, wo), (wus, wu), (wds, wd))):
        shared[k].wait_recv()
        local[4 + k].wait()
        copy(a, b)
    for cp in outs:
        cp.wait_recv()
    w.drain()
    for cp in local[7:]:
        cp.wait()


def front(nz, order, vectors, x, weights):
    A = pl.BlockSpec(memory_space=pltpu.HBM)
    V = pl.BlockSpec(memory_space=pltpu.VMEM)
    sds = jax.ShapeDtypeStruct
    M = pltpu.VMEM
    rows, dim = x.shape[1:]
    wq, wk, wv, wo, wu, wd = weights
    outs = [sds((2, rows, dim), bf16)] + [sds((2 * w.shape[0], w.shape[1]), bf16) for w in (wo, wu, wd)]
    outs += [sds((2, 16, 256), f32), sds((nz, 4, rows, dim), bf16), sds((dim, 768), bf16)] + list(fwd_outs(nz)[1:])
    scratch = [M((nz, 4, rows, dim), bf16), M((dim, 768), bf16), M((2, 16, 256), f32)] + [M(o.shape, bf16) for o in outs[1:4]]
    scratch += [M((nz, 2, 512, 256), bf16)] * 2 + [M((nz, 2, 256, 512), bf16)] * 2 + [M((4, 2, 128, 256), bf16), M((4, 2, 256, 128), bf16)]
    scratch += fwd_scratch(nz)[1:] + [M((256, 1), f32), M((4, 2, 256, 128), f32), M((4, 2, 1, 512), f32), M((4, 256, 256), bf16)]
    scratch += [pltpu.SemaphoreType.DMA((40,)), pltpu.SemaphoreType.DMA((40,)), pltpu.SemaphoreType.DMA((40,))]
    return pl.pallas_call(
        functools.partial(front_kernel, nz), out_shape=tuple(outs),
        in_specs=[pl.BlockSpec(memory_space=pltpu.SMEM)] + [V] * 9 + [A] * 7, out_specs=(A,) * len(outs), scratch_shapes=scratch,
        compiler_params=pltpu.CompilerParams(collective_id=1, has_side_effects=True, vmem_limit_bytes=58 << 20), name="front")(
            order, *vectors, x, *weights)


def back_kernel(nz, order_ref, gv_ref, do_ref, x_hbm, w_hbm, K_h, V_h, KT_h, qn_h, qt_h, ot_h, lse_h, gw_ref,
                dxo, go, gqo, gvo,
                xs, wqkv, K, V, KT, qn, qt, ot, lse, do, qs, dos, qns, dons, dl, dk, dv, dq, d_s, gb, dxq, dw, dx, gp, gq, db, outdx,
                dx_core, dx_in, cr, cs, xr, xs_, yr, ys_, za, zs, zb, xrq, xsq, yrq, ysq, zrq, gsum, gqsum, gvs, gvr, send, recv, lsem):
    me, wi, z, y, c, low, to = places(nz)
    to["yc"] = (z * 4 + 3 - low, wi)
    zto = [(lax.rem(z + d, nz) * 4 + low, wi) for d in range(1, nz)]
    half, hrow = 256, 256
    w = Wires(send, recv)
    local = []

    def copy(src, dst):
        cp = pltpu.make_async_copy(src, dst, lsem.at[len(local)])
        cp.start()
        local.append(cp)
        return cp

    cols = pl.ds(pl.multiple_of(c * half, half), half)
    other = pl.ds(pl.multiple_of((1 - c) * half, half), half)
    meet([to[k] for k in ("core", "y", "yc", "x")] + zto)
    dos_in = [w.go(do_ref.at[1 - y, :, cols], do.at[2], to["y"]), w.go(do_ref.at[1 - y, :, other], do.at[3], to["yc"]),
              w.go(do_ref.at[y, :, other], do.at[1], to["core"])]
    got = {}
    for s in range(3):
        got["c", s] = w.go(gw_ref.at[:, rows_of(s * 768 + (1 - c) * 384, 384)], cr.at[s], to["core"])
    mine_gw = [copy(gw_ref.at[:, rows_of(s * 768 + c * 384, 384)], cs.at[s]) for s in range(3)]
    first_in = [copy(do_ref.at[y, :, cols], do.at[0])] + [copy(a, b) for a, b in ((qn_h, qn), (qt_h, qt), (ot_h, ot), (lse_h, lse))]
    kv_in = {}
    for r in list(range(1, nz)) + [0]:
        kv_in[r] = [copy(a.at[r], b.at[r]) for a, b in ((K_h, K), (V_h, V), (KT_h, KT), (x_hbm, xs))]
    w_in = copy(w_hbm, wqkv)

    n = range(5)
    wide = [384, 192, 48]
    zp = (z + 1 - 2 * lax.rem(z, 2)) * 4 + low, wi
    zq = (z + 2 - 4 * (z // 2)) * 4 + low, wi
    odd, far = lax.rem(z, 2), z // 2
    X_in = [xr.at[s] for s in range(3)] + [xrq.at[s] for s in range(2)]
    X_sum = [xs_.at[s] for s in range(3)] + [xsq.at[s] for s in range(2)]
    Y_in = [yr.at[s] for s in range(3)] + [yrq.at[s] for s in range(2)]
    Y_sum = [ys_.at[s] for s in range(3)] + [ysq.at[s] for s in range(2)]
    Z_in = [zrq.at[s] for s in range(2)]
    out = [gsum.at[s] for s in range(3)] + [gqsum.at[s] for s in range(2)]
    start_c, start_y = c * 384, c * 384 + y * 192
    at_c, at_y = rows_of(start_c, 384), rows_of(start_y, 192)
    pos = odd * 2 + far
    start_p, start_h = start_y + pos * 48, start_y + odd * 96
    at_p, at_h = rows_of(start_p, 48), rows_of(start_h, 96)
    start_z = start_y + z * 48
    at_z = rows_of(start_z, 48)
    theirs = rows_of((1 - y) * 192, 192)
    for s in n:
        got["x", s] = w.make(cs.at[s, 1 - wi] if s < 3 else gq.at[1 - wi, pl.ds((s - 3) * 384, 384)], X_in[s], to["x"])
        got["y", s] = w.make(X_sum[s].at[theirs], Y_in[s], to["y"])
        got["ys", s] = w.make(out[s].at[at_y], out[s].at[at_y], to["y"])
        got["cs", s] = w.make(out[s].at[at_c], out[s].at[at_c], to["core"])
        if s < 3:
            got["za", s] = w.make(ys_.at[s, rows_of((1 - odd) * 96, 96)], za.at[s], zp)
            got["zb", s] = w.make(zs.at[s, rows_of((1 - far) * 48, 48)], zb.at[s], zq)
            got["zc", s] = w.make(out[s].at[at_p], out[s].at[at_p], zq)
            got["zd", s] = w.make(out[s].at[at_h], out[s].at[at_h], zp)
        else:
            for d in range(1, nz):
                got["z", s, d] = w.make(Y_sum[s].at[rows_of(lax.rem(z + d, nz) * 48, 48)], Z_in[s - 3].at[d - 1], zto[d - 1])
                got["zs", s, d] = w.make(out[s].at[at_z], out[s].at[at_z], zto[d - 1])

    def x_send(s):
        if s < 3:
            mine_gw[s].wait()
            got["c", s].wait_recv()
            add_into(offset(cs, (s, 1 - wi), 0), [offset(cs, (s, 1 - wi), 0), offset(cr, (s, 1 - wi), 0)], 384, 128)
            got["x", s].start()
            add_into(offset(cs, (s, wi), 0), [offset(cs, (s, wi), 0), offset(cr, (s, wi), 0)], 384, 128)
        else:
            got["x", s].start()

    def y_send(s):
        got["x", s].wait_recv()
        mine = lambda lo: offset(cs, (s, wi), lo) if s < 3 else offset(gq, (wi,), (s - 3) * 384 + lo)
        for half_y in (1 - y, y):
            lo = half_y * 192
            add_into(offset(X_sum[s], (), lo), [mine(lo), offset(X_in[s], (), lo)], 192, 96)
            if half_y is not y:
                got["y", s].start()

    def z_a(s):
        got["y", s].wait_recv()
        add_into(offset(ys_, (s,), 0), [offset(xs_, (s,), y * 192), offset(yr, (s,), 0)], 192, 96)
        got["za", s].start()

    def z_b(s):
        got["za", s].wait_recv()
        add_into(offset(zs, (s,), 0), [offset(ys_, (s,), odd * 96), offset(za, (s,), 0)], 96, 96)
        got["zb", s].start()

    def z_c(s):
        got["zb", s].wait_recv()
        add_into(offset(out[s], (), start_p), [offset(zs, (s,), far * 48), offset(zb, (s,), 0)], 48, 48)
        got["zc", s].start()

    def z_d(s):
        got["zc", s].wait_recv()
        got["zd", s].start()

    def z_send(s):
        got["y", s].wait_recv()
        add_into(offset(Y_sum[s], (), 0), [offset(X_sum[s], (), y * 192), offset(Y_in[s], (), 0)], 192, 192)
        for d in range(1, nz):
            got["z", s, d].start()

    def z_share(s):
        for d in range(1, nz):
            got["z", s, d].wait_recv()
        add_into(offset(out[s], (), start_z), [offset(Y_sum[s], (), z * 48)] + [offset(Z_in[s - 3], (d,), 0) for d in range(nz - 1)], 48, 48)
        for d in range(1, nz):
            got["zs", s, d].start()

    def y_share(s):
        for k in (["zd"] if s < 3 else [("zs", d) for d in range(1, nz)]):
            got[(k, s) if s < 3 else (k[0], s, k[1])].wait_recv()
        got["ys", s].start()

    def c_share(s):
        got["ys", s].wait_recv()
        got["cs", s].start()

    for r in range(nz):
        for h in range(2):
            at = pl.ds(h * 512, hrow)
            got["d", r, h] = w.make(dx.at[r, pl.ds(h * 512 + hrow, hrow)], dx_core.at[r, h], to["core"])
            if r:
                got["r", (r + 1) % nz, h] = w.make(dx.at[r, at], dx_in.at[(r + 1) % nz, h], to["up"])
    got["dy"] = w.make(dx.at[0, pl.ds(512, hrow)], outdx.at[1], to["y"])

    def give(r, h):
        got["d", r, h].start()

    def fold(r, h):
        got["d", r, h].wait_recv()
        add_into(offset(dx, (r,), h * 512), [offset(dx, (r,), h * 512), offset(dx_core, (r, h), 0)], hrow, 128)
        if r == 1:
            got["r", 2, h].start()

    def hop(r, h):
        got["r", r, h].wait_recv()
        dst = offset(dx, (r,), h * 512) if r or h else offset(outdx, (0,), 0)
        add_into(dst, [offset(dx, (r,), h * 512), offset(dx_in, (r, h), 0)], hrow, 128)
        if r:
            got["r", (r + 1) % nz, h].start()
        elif h:
            got["dy"].start()

    vec_to = [to["core"], to["y"], to["x"]] + [(zz * 4 + low, wi) for zz in (z + 1 - 2 * lax.rem(z, 2), z + 2 - 4 * (z // 2))]

    def vec_send(k):
        if k == 0:
            gvs[0] = jnp.zeros_like(gvs[0])
            gvs[0, 0:16, :] = gv_ref[...]
            zero = jnp.zeros((1, half), f32)
            for i in range(2):
                v = db[i:i + 1, :]
                gvs[0, 16 + i:17 + i, :] = jnp.concatenate([jnp.where(c == 0, v, zero), jnp.where(c == 0, zero, v)], axis=1)
        else:
            got["v", k - 1].wait_recv()
            gvs[k] = gvs[k - 1] + gvr[k - 1]
        if k < 5:
            got["v", k].start()
        else:
            gvo[...] = gvs[5]

    pairs = chip_pairs(nz, order_ref)
    for k in range(5):
        got["v", k] = w.make(gvs.at[k], gvr.at[k], vec_to[k])
    diagonal(d_s)
    dw[...] = jnp.zeros_like(dw)
    db[...] = jnp.zeros_like(db)
    for s in (qs, dos, qns, dons):
        s[...] = jnp.zeros_like(s)
    x_send(0)
    for cp in first_in:
        cp.wait()
    for cp in dos_in:
        cp.wait_recv()
    bwd_queries(pairs, do, ot, qn, qt, qs, dos, qns, dons, dl)
    for r in kv_in:
        for cp in kv_in[r]:
            cp.wait()
    w_in.wait()
    hooks = plan(dict(x=x_send, y=y_send, za=z_a, zb=z_b, zc=z_c, zd=z_d, ys=y_share, cs=c_share, fold=fold, hop=hop, z=z_send, zs=z_share, vec=vec_send))
    hook = lambda *k: hooks[k]() if k in hooks else None
    hook("pre")
    for r in list(range(1, nz)) + [0]:
        dk[...] = jnp.zeros_like(dk)
        dv[...] = jnp.zeros_like(dv)
        for n, js in enumerate(((2, 3), (0, 1)) if r == 1 else ((0, 1, 2, 3),)):
            def step(i, _):
                bwd_step(pairs, r, i, r == 0, r == 1 and n == 0, K, V, KT, qs, dos, qns, dons, lse, dl, dk, dv, dq, d_s, gb, js)
                for k in range(4):
                    if (r, n, k) in hooks:
                        pl.when(i == k)(hooks[r, n, k])
                return 0
            lax.fori_loop(0, 4, step, 0)
            if r == 0:
                bwd_query_out(pairs, xs, wqkv, dq, dxq, dw, db)
                hook(0, 0, "q")
            bwd_chunk_weights(pairs, r, xs, dk, dv, dw, db, gp, js)
            if r == 0:
                weight_rows(dw, gq)
                x_send(3)
            hook(r, n, "w")
            bwd_chunk_rows(r, r == 0, wqkv, dxq, dx, gp, [p for p in (3, 1, 2, 0) if p in js])
            for h in (1, 0):
                if 2 * h in js:
                    give(r, h)
            hook(r, n, "r")
    hook("tail")
    for s in range(5):
        got["cs", s].wait_recv()
        copy(gsum.at[s], go.at[s]) if s < 3 else copy(gqsum.at[s - 3], gqo.at[s - 3])
    got["dy"].wait_recv()
    copy(outdx, dxo)
    w.drain()
    for cp in local[-6:]:
        cp.wait()


PLAN = {
    (1, 0, "r"): (("x", 2),),
    (1, 1, 2): (("y", 0),),
    (1, 1, "r"): (("fold", 1, 1),),
    (2, 0, 2): (("x", 1), ("fold", 1, 0), ("za", 0),),
    (2, 0, "r"): (("y", 2),),
    (3, 0, 2): (("zb", 0),),
    (3, 0, 3): (("za", 2), ("fold", 2, 0), ("y", 1),),
    (3, 0, "r"): (("zc", 0), ("hop", 2, 0),),
    (0, 0, 2): (("za", 1),),
    (0, 0, "q"): (("zb", 2), ("zd", 0), ("fold", 2, 1),),
    (0, 0, "w"): (("hop", 2, 1), ("zc", 2), ("vec", 0), ("zb", 1), ("fold", 3, 1), ("fold", 3, 0), ("y", 3), ("x", 4), ("zd", 2), ("zc", 1), ("ys",
        0), ("z", 3), ("y", 4),),
    (0, 0, "r"): (("zd", 1), ("fold", 0, 1), ("hop", 3, 1), ("zs", 3), ("ys", 2), ("z", 4),),
    "tail": (("fold", 0, 0), ("vec", 1), ("ys", 1), ("ys", 3), ("vec", 2), ("cs", 0), ("zs", 4), ("vec", 3), ("hop", 3, 0), ("cs", 2), ("hop", 0, 1),
        ("cs", 1), ("ys", 4), ("cs", 3), ("vec", 4), ("cs", 4), ("vec", 5), ("hop", 0, 0),),
}


def plan(ops):
    def run(items):
        def go():
            for name, *a in items:
                ops[name](*a)
        return go
    return {k if isinstance(k, tuple) else (k,): run(v) for k, v in PLAN.items()}


def back(nz, order, gv, do, x_all, wqkv, k, v, kt, qn, qt, ot, lse, gw):
    A = pl.BlockSpec(memory_space=pltpu.HBM)
    V = pl.BlockSpec(memory_space=pltpu.VMEM)
    sds = jax.ShapeDtypeStruct
    B = lambda *s: pltpu.VMEM(s, bf16)
    F = lambda *s: pltpu.VMEM(s, f32)
    ins = (x_all, wqkv, k, v, kt, qn, qt, ot, lse)
    scratch = [pltpu.VMEM(a.shape, a.dtype) for a in ins] + [B(4, 256, 256)] + bwd_scratch()
    scratch += [B(nz, 1024, 512), B(1024, 512), B(2, 768, 256), F(8, 256), B(2, 256, 512)]
    scratch += [B(nz, 2, 256, 512), B(nz, 2, 256, 512), B(3, 2, 384, 512), B(3, 2, 384, 512), B(3, 384, 512), B(3, 384, 512), B(3, 192, 512), B(3, 192, 512),
                B(3, 96, 512), B(3, 96, 512), B(3, 48, 512), B(2, 384, 256), B(2, 384, 256), B(2, 192, 256), B(2, 192, 256), B(2, nz - 1, 48, 256),
                B(3, 768, 512), B(2, 768, 256),
                F(6, 24, 512), F(5, 24, 512)]
    scratch += [pltpu.SemaphoreType.DMA((80,)), pltpu.SemaphoreType.DMA((80,)), pltpu.SemaphoreType.DMA((40,))]
    return pl.pallas_call(
        functools.partial(back_kernel, nz),
        out_shape=(sds((2, 256, 512), bf16), sds((3, 768, 512), bf16), sds((2, 768, 256), bf16), sds((24, 512), f32)),
        in_specs=[pl.BlockSpec(memory_space=pltpu.SMEM), V] + [A] * 11, out_specs=(A, A, A, V), scratch_shapes=scratch,
        compiler_params=pltpu.CompilerParams(collective_id=2, has_side_effects=True, vmem_limit_bytes=62 << 20), name="back")(order, gv, do, *ins, gw)


def last_kernel(nu, go_ref, gq_ref, gv_ref, dx_ref, dsm_ref, gin, dwq, dbq, dwk, dwv, dbv, dwo, dbo, dg1, ds1, dwu, dbu, dwd, dbd, dg2, ds2):
    wi, y = lax.axis_index("wt"), lax.rem(lax.axis_index("ctx") // 2, 2)
    for s in range(2):
        seq = jnp.where(y == 0, s, 1 - s)
        gin[s] = (dsm_ref[s] + dx_ref[seq].astype(f32)).astype(bf16)
    hr = dwq.shape[0]
    for k in range(2):
        at, low = slice(k * 256, k * 256 + 256), k * 384
        dwq[:, at] = gq_ref[0, low:low + 256, :].astype(f32)
        dwk[0:128, at] = gq_ref[0, low + 256:low + 384, :].astype(f32)
        dwk[128:256, at] = gq_ref[1, low:low + 128, :].astype(f32)
        dwv[:, at] = gq_ref[1, low + 128:low + 384, :].astype(f32)
    dwo[...] = go_ref[0:hr, :].astype(f32)
    for k in range(nu):
        dwu[:, k * 512:k * 512 + 512] = go_ref[hr + k * hr:2 * hr + k * hr, :].astype(f32)
    dwd[...] = go_ref[hr + nu * hr:, :].astype(f32)

    def row(i):
        v = gv_ref[i:i + 1, :]
        return jnp.where(wi == 0, v[:, :256], v[:, 256:])

    for o, i in ((dbo, 0), (dg1, 1), (ds1, 2), (dbd, 3), (dg2, 4), (ds2, 5), (dbq, 16), (dbv, 17)):
        o[...] = row(i).reshape(256)
    h = nu // 2
    a, b = [jnp.concatenate([gv_ref[8 + k * h + i:9 + k * h + i, :] for i in range(h)], axis=1) for k in range(2)]
    dbu[...] = jnp.where(wi == 0, a, b).reshape(a.shape[1])


def last(nu, go, gqo, gv, dxo, dsm):
    V = pl.BlockSpec(memory_space=pltpu.VMEM)
    f = lambda *s: jax.ShapeDtypeStruct(s, f32)
    ff = nu * 512
    outs = (jax.ShapeDtypeStruct((2, 256, 512), bf16), f(256, 512), f(256), f(256, 512), f(256, 512), f(256), f(256, 512), f(256), f(256), f(256),
            f(256, ff), f(ff // 2), f(ff // 2, 512), f(256), f(256), f(256))
    return pl.pallas_call(functools.partial(last_kernel, nu), out_shape=outs, in_specs=[V] * 5, out_specs=(V,) * 16,
                          compiler_params=pltpu.CompilerParams(vmem_limit_bytes=56 << 20), name="last")(go, gqo, gv, dxo, dsm)


def body(block_in, block_order, w_query, b_query, w_key, w_value, b_value, w_out, b_out, gain_one, shift_one,
         w_up, b_up, w_down, b_down, gain_two, shift_two, cotangent, *, nc, nw):
    seqs, rows, dim = block_in.shape
    nz = nc // 4
    hb = rows // BLOCK
    half = dim // 2
    me = lax.axis_index("ctx")
    yy = (me // 2) % 2
    cc = me % 2
    zz = me // 4
    xor = lambda v: [(i, i ^ v) for i in range(nc)]
    ring = [(i, ((i // 4 + 1) % nz) * 4 + i % 4) for i in range(nc)]
    perm = lambda v, p: lax.ppermute(v, "ctx", p)
    gather = lambda v: lax.all_gather(v, "wt", axis=0, tiled=True)
    pick = lambda v, i: lax.dynamic_index_in_dim(v, i, 0, keepdims=False)

    ours = nw == 2 and nz == 4
    small = (b_query, b_value, b_out, gain_one, shift_one, b_down, gain_two, shift_two, b_up)
    by_seq = lambda a, b: jnp.where(yy == 0, jnp.concatenate([a, b], 0), jnp.concatenate([b, a], 0))
    r_ids = (zz - jnp.arange(nz, dtype=jnp.int32)) % nz
    quad = (me % 4) ^ jnp.array([0, 1, 2, 3], jnp.int32)
    order_row = pick(block_order, yy)
    slots = (r_ids[:, None, None] * 4 + quad[None, :, None]) * hb + jnp.arange(hb, dtype=jnp.int32)
    blk = order_row[slots.reshape(-1)]

    if ours:
        att, wo, wu, wd, sm, x_all, wqkv, ot, lse, k, v, kt, qn, qt = front(nz, block_order, small, block_in, (w_query, w_key, w_value, w_out, w_up, w_down))
        att = att.reshape(-1, dim)
    else:
        cols = lambda w: lax.dynamic_slice_in_dim(w, cc * half, half, 1)
        wqkv = gather(jnp.concatenate([cols(w_query), cols(w_key), cols(w_value)], axis=1))
        small = lax.all_gather(jnp.concatenate(small), "wt", axis=0)
        vec8 = jnp.transpose(small[:, :8 * dim // nw].reshape(nw, 8, dim // nw), (1, 0, 2)).reshape(8, 2, half)
        upb = small[:, 8 * dim // nw:].reshape(2, 4, half)
        sm = jnp.pad(jnp.concatenate([jnp.transpose(vec8, (1, 0, 2)), upb], axis=1).astype(f32), ((0, 0), (0, 4), (0, 0)))
        wo, wu, wd = gather(w_out), gather(w_up), gather(w_down)
        x_all = gather_all(nz, block_in)[0]
        o, ot, lse, k, v, kt, qn, qt = attn_fwd(nz, blk, x_all, wqkv, pick(sm, cc)[0:1], pick(sm, cc)[1:2])
        o_self, o_c, o_y, o_yc = o[0], perm(o[1], xor(1)), perm(o[2], xor(2)), perm(o[3], xor(3))
        mine, other = by_seq(o_self, o_y), by_seq(o_c, o_yc)
        att = jnp.where(cc == 0, jnp.concatenate([mine, other], 1), jnp.concatenate([other, mine], 1))

    out, dsm, d_o, gw, gv = dense(block_in.reshape(-1, dim), cotangent.reshape(-1, dim), att, wo, wu, wd, sm)

    if ours:
        dxo, go, gqo, gvec = back(nz, block_order, gv, d_o.reshape(seqs, rows, dim), x_all, wqkv, k, v, kt, qn, qt, ot, lse, gw)
        return (out.reshape(seqs, rows, dim),) + tuple(last(w_up.shape[1] // dim, go.reshape(-1, dim), gqo, gvec, dxo, dsm.reshape(seqs, rows, dim)))
    d_o = d_o.reshape(seqs, rows, dim)
    d_own, d_oth = pick(d_o, yy), pick(d_o, 1 - yy)
    fh = lambda v, c: lax.dynamic_slice_in_dim(v, c * half, half, 1)
    do_all = jnp.concatenate([fh(d_own, cc), perm(fh(d_own, 1 - cc), xor(1)), perm(fh(d_oth, cc), xor(2)), perm(fh(d_oth, 1 - cc), xor(3))], axis=0)
    dx, gq, gb = attn_bwd(nz, blk, x_all, wqkv, k, v, kt, qn, qt, ot, lse, do_all.reshape(4, rows, half))
    gvec = jnp.zeros((24, dim), f32).at[:16].set(gv)
    gvec = lax.dynamic_update_slice(gvec, gb[0:1], (16, cc * half))
    gvec = lax.dynamic_update_slice(gvec, gb[1:2], (17, cc * half))
    wi = lax.axis_index("wt")
    ff, hr = w_up.shape[1], dim // 2
    nu = ff // dim
    dx = jnp.transpose(dx.reshape(nz, 2, 2, rows, dim), (0, 2, 1, 3, 4)).reshape(nz, 2, 2 * rows, dim)
    part = lambda r: dx[r, 0].astype(f32) + perm(dx[r, 1], xor(1)).astype(f32)
    acc = None
    for r in list(range(1, nz)) + [0]:
        acc = part(r) if acc is None else perm(acc.astype(bf16), ring).astype(f32) + part(r)
    from_y = perm(acc[rows:].astype(bf16), xor(2)).astype(f32)
    dkv_sum = by_seq(acc[:rows], from_y)
    gvec = lax.psum(gvec, ("ctx", "wt"))
    g_out = gw[:, :hr].reshape(dim, dim)
    g_up = gw[:, hr:hr + nu * hr].reshape(2, nu, hr, dim).transpose(0, 2, 1, 3).reshape(dim, ff)
    g_down = gw[:, hr + nu * hr:].reshape(ff, dim)
    gq3 = gq.reshape(2, 3, hr, half).transpose(1, 0, 2, 3).reshape(3, dim, half)
    g_qkv = lax.dynamic_update_slice(jnp.zeros((3, dim, dim), bf16), gq3, (0, 0, cc * half))
    total = lambda g: lax.psum(lax.psum_scatter(g, "wt", scatter_dimension=0, tiled=True), "ctx").astype(f32)
    t_out, t_up, t_down = total(g_out), total(g_up), total(g_down)
    t_qkv = [total(g_qkv[i]) for i in range(3)]
    grad_in = (dsm + dkv_sum).astype(bf16).reshape(seqs, rows, dim)

    def share(vv):
        n = vv.size // nw
        return lax.dynamic_slice_in_dim(vv.reshape(-1), wi * n, n, 0)
    return (out.reshape(seqs, rows, dim), grad_in, t_qkv[0], share(gvec[16]), t_qkv[1], t_qkv[2], share(gvec[17]), t_out, share(gvec[0]),
            share(gvec[1]), share(gvec[2]), t_up, share(gvec[8:8 + nu]), t_down, share(gvec[3]), share(gvec[4]), share(gvec[5]))


def solution(mesh):
    seq, mat, vec = P("wt", "ctx", None), P("wt", None), P("wt")
    ins = (seq, mat, mat, vec, mat, mat, vec, mat, vec, vec, vec, mat, vec, mat, vec, vec, vec, seq)
    outs = (seq, seq, mat, vec, mat, mat, vec, mat, vec, vec, vec, mat, vec, mat, vec, vec, vec)
    run = functools.partial(body, nc=mesh.shape["ctx"], nw=mesh.shape["wt"])
    return jax.shard_map(run, mesh=mesh, in_specs=ins, out_specs=outs, check_vma=False)
```

profile of v0, /device:TPU:0, one launch (start us, length us, event | category | flops | bytes accessed | tf_op | source)
XLA Modules:
  0.0 180.0 jit_solution(18022073671316441180)
XLA Ops:
  0.7 59.7 %front.1 = (bf16[2,256,512]{2,1,0:T(8,128)(2,1)}, bf16[512,512]{1,0:T(8,128)(2,1)}, bf16[512,2048]{1,0:T(8,128)(2,1)}, bf16[2048,512]{1,0:T(8,128)(2,1)}, f32[2,...) custom-call(s32[2,32]{1,0:T(2,128)} %order_ref.3, ...), custom_call_target="tpu_custom_call" | custom-call | tf_op jit(solution)/shard_map/front/pallas_call | solution.py:728
  60.3 14.7 %dense.1 = (bf16[512,512]{1,0:T(8,128)(2,1)}, f32[512,512]{1,0:T(8,128)}, bf16[512,512]{1,0:T(8,128)(2,1)}, bf16[2,2304,512]{2,1,0:T(8,128)(2,1)}, f32[16,512]{1,0:T(8,128)}) custom-call(bf16[512,512]{1,0:T(8,128)(2,1)} %bitcast.8, bf16[512,512]{1,0:T(8,128)(2,1)} %bitcast.10, bf16[512,512]{1,0:T(8,128)(2,1)} %bitcast.12, ...), custom_call_target="tpu_custom_call" | custom-call | tf_op jit(solution)/shard_map/dense/pallas_call | solution.py:420
  75.0 99.5 %back.1 = (bf16[2,256,512]{2,1,0:T(8,128)(2,1)}, bf16[3,768,512]{2,1,0:T(8,128)(2,1)}, bf16[2,768,256]{2,1,0:T(8,128)(2,1)}, f32[24,512]{1,0:T(8,128)}) custom-call(s32[2,32]{1,0:T(2,128)} %order_ref.3, f32[16,512]{1,0:T(8,128)} %get-tuple-element.62.gv_ref, bf16[2,256,512]{2,1,0:T(8,128)(2,1)} %bitcast.11, ...), custom_call_target="tpu_custom_call" | custom-call | tf_op jit(solution)/shard_map/back/pallas_call | solution.py:1003
  174.5 5.3 %last.1 = (bf16[2,256,512]{2,1,0:T(8,128)(2,1)}, f32[256,512]{1,0:T(8,128)}, f32[256]{0:T(256)}, f32[256,512]{1,0:T(8,128)}, f32[256,512]{1,0:T(8,128)}, /*index...) custom-call(bf16[2304,512]{1,0:T(8,128)(2,1)} %bitcast.7, ...), custom_call_target="tpu_custom_call" | custom-call | tf_op jit(solution)/shard_map/last/pallas_call | solution.py:1044
where the time goes:
time: 180 us
  Pallas kernels  179 us (99%)
    pallas_call x1, Pallas kernels, back(): pl.pallas_call(functools.partial(back_kernel, nz), out_shape=(sds((2, 256...  99.5 us
    pallas_call x1, Pallas kernels, front(): pl.pallas_call(functools.partial(front_kernel, nz), out_shape=tuple(outs)...  59.7 us
    pallas_call x1, Pallas kernels, dense(): pl.pallas_call(dense_kernel, out_shape=(jax.ShapeDtypeStruct((tok, dim),...  14.7 us
    pallas_call x1, Pallas kernels, last(): pl.pallas_call(functools.partial(last_kernel, nu), out_shape=outs, in_spe...  5.32 us

commit v1 on v0

--- a/solution.py
+++ b/solution.py
@@ -48,7 +48,7 @@
         return jnp.where(first, a, b), jnp.where(first, b, a)
 
 
-def project_chunk(pairs, r, x_ref, wkv_ref, wkvt_ref, bkv_ref, bkvt_ref, K, V, KT, VT):
+def project_chunk(pairs, r, x_ref, wkv_ref, wkvt_ref, bkv_ref, bkvt_ref, K, V, KT, VT, start=0, stop=4):
     def piece(p, _):
         x = jnp.concatenate(pairs.ordered(r * 4 + p, x_ref[r, p]), axis=0)
         kv = dot(x, wkv_ref[...])
@@ -63,7 +63,7 @@
             KT[r, u, :, at] = kt[:, rows]
             VT[r, u, :, at] = vt[:, rows]
         return 0
-    lax.fori_loop(0, 4, piece, 0)
+    lax.fori_loop(start, stop, piece, 0)
 
 
 def project_queries(pairs, x_ref, wq_ref, bq_ref, qn, qt, qs):
@@ -91,21 +91,22 @@
     return jnp.concatenate([a[64 * (h % 2):64 * (h % 2) + 64, 128 * h:128 * h + 128] for h in range(HEADS_HERE)], axis=0)
 
 
-def fwd_step(pairs, r, i, own, K, VT, qs, m_s, l_s, acc, d_s, sb, pb):
+def fwd_step(pairs, r, i, own, K, VT, qs, m_s, l_s, acc, d_s, sb, pb, js=(0, 1, 2, 3)):
+    part = slice(js[0] * BLOCK, js[-1] * BLOCK + BLOCK)
     col = lambda v: jnp.max(v, axis=0, keepdims=True)
     tot = lambda v: jnp.sum(v, axis=0, keepdims=True)
     lo_i = pairs.lo(i)
-    pick = [lo_i > pairs.lo(r * 4 + j) for j in range(4)]
-    sa = dot(K[r, 0], qs[i, 1])
-    for j in range(4):
+    pick = {j: lo_i > pairs.lo(r * 4 + j) for j in js}
+    sa = dot(K[r, 0, part, :], qs[i, 1])
+    for j in js:
         u = jnp.where(pick[j], 0, 1)
         s = dot(K[r, u, j * BLOCK:(j + 1) * BLOCK, :], qs[i, u])
         if own:
             s = jnp.where(d_s[...] <= jnp.where(i == j, 0, 2 * BLOCK), s, FAR)
         sb[j] = s
-    tops = [col(sb[j]) for j in range(4)]
+    tops = {j: col(sb[j]) for j in js}
     m_hi, m_lo = col(sa), None
-    for j in range(4):
+    for j in js:
         m_hi = jnp.maximum(m_hi, jnp.where(pick[j], FAR, tops[j]))
         t = jnp.where(pick[j], tops[j], FAR)
         m_lo = t if m_lo is None else jnp.maximum(m_lo, t)
@@ -118,7 +119,7 @@
         m_hi, m_lo = jnp.maximum(m_hi, old_hi), jnp.maximum(m_lo, old_lo)
     pa = jnp.exp2(sa - m_hi)
     l_hi, l_lo = tot(pa), jnp.zeros((1, 512), f32)
-    for j in range(4):
+    for j in js:
         p = jnp.exp2(sb[j] - jnp.where(pick[j], m_lo, m_hi))
         t = tot(p)
         l_hi = l_hi + jnp.where(pick[j], 0.0, t)
@@ -128,8 +129,8 @@
         zero = jnp.zeros_like(low)
         pb[0, rows, :] = jnp.where(pick[j], low, zero)
         pb[1, rows, :] = jnp.where(pick[j], zero, low)
-    o_hi = by_pair(VT[r, 0], pa.astype(bf16)) + by_pair(VT[r, 1], pb[1])
-    o_lo = by_pair(VT[r, 0], pb[0])
+    o_hi = by_pair(VT[r, 0, :, part], pa.astype(bf16)) + by_pair(VT[r, 1, :, part], pb[1, part, :])
+    o_lo = by_pair(VT[r, 0, :, part], pb[0, part, :])
     if own:
         p = jnp.exp2(sd - m_lo)
         l_lo = l_lo + tot(p)
@@ -146,20 +147,17 @@
     m_s[i, 1], m_s[i, 0] = m_hi, m_lo
 
 
-def fwd_finish(pairs, m_s, l_s, acc, lse, ot, o_ref):
-    def pair(i, _):
-        first = pairs.first_lo(i)
-        out = []
-        for u in range(2):
-            l = l_s[i, u]
-            lse[i, u] = m_s[i, u] + jnp.log2(l)
-            t = unpair(acc[i, u] * (1.0 / l))
-            ot[i, u] = t
-            out.append(t.T.astype(bf16))
-        o_ref[i, 0:BLOCK, :] = jnp.where(first, out[0], out[1])
-        o_ref[i, BLOCK:2 * BLOCK, :] = jnp.where(first, out[1], out[0])
-        return 0
-    lax.fori_loop(0, 4, pair, 0)
+def fwd_finish(pairs, i, m_s, l_s, acc, lse, ot, o_ref):
+    first = pairs.first_lo(i)
+    out = []
+    for u in range(2):
+        l = l_s[i, u]
+        lse[i, u] = m_s[i, u] + jnp.log2(l)
+        t = unpair(acc[i, u] * (1.0 / l))
+        ot[i, u] = t
+        out.append(t.T.astype(bf16))
+    o_ref[i, 0:BLOCK, :] = jnp.where(first, out[0], out[1])
+    o_ref[i, BLOCK:2 * BLOCK, :] = jnp.where(first, out[1], out[0])
 
 
 def diagonal(d_s):
@@ -177,7 +175,8 @@
             fwd_step(pairs, r, i, r == 0, K, VT, qs, m_s, l_s, acc, d_s, sb, pb)
             return 0
         lax.fori_loop(0, 4, step, 0)
-    fwd_finish(pairs, m_s, l_s, acc, lse, ot, o_ref)
+    for i in range(4):
+        fwd_finish(pairs, i, m_s, l_s, acc, lse, ot, o_ref)
 
 
 def fwd_outs(nz):
@@ -201,21 +200,18 @@
         compiler_params=pltpu.CompilerParams(vmem_limit_bytes=58 << 20), name="attn_fwd")(blk, x, wqkv, bq, bkv, bkv.reshape(256, 1))
 
 
-def bwd_queries(pairs, do_ref, ot, qn, qt, qs, dos, qns, dons, dl):
-    def piece(i, _):
-        for u, do in enumerate(pairs.ordered(i, do_ref[i])):
-            dot_t = do.astype(f32).T
-            prod = dot_t * ot[i, u]
-            low = dot_t.astype(bf16)
-            q, t = qn[i, u], qt[i, u]
-            for hs, cs in head_slices():
-                qs[i, u, hs, cs] = t[hs]
-                dos[i, u, hs, cs] = low[hs]
-                qns[i, u, cs, hs] = q[:, hs]
-                dons[i, u, cs, hs] = do[:, hs]
-                dl[i, u, :, cs] = jnp.sum(prod[hs], axis=0, keepdims=True)
-        return 0
-    lax.fori_loop(0, 4, piece, 0)
+def bwd_query(pairs, i, do_ref, ot, qn, qt, qs, dos, qns, dons, dl):
+    for u, do in enumerate(pairs.ordered(i, do_ref[i])):
+        dot_t = do.astype(f32).T
+        prod = dot_t * ot[i, u]
+        low = dot_t.astype(bf16)
+        q, t = qn[i, u], qt[i, u]
+        for hs, cs in head_slices():
+            qs[i, u, hs, cs] = t[hs]
+            dos[i, u, hs, cs] = low[hs]
+            qns[i, u, cs, hs] = q[:, hs]
+            dons[i, u, cs, hs] = do[:, hs]
+            dl[i, u, :, cs] = jnp.sum(prod[hs], axis=0, keepdims=True)
 
 
 def bwd_step(pairs, r, i, own, first, K, V, KT, qs, dos, qns, dons, lse, dl, dk, dv, dq, d_s, gb, js=(0, 1, 2, 3)):
@@ -310,7 +306,8 @@
     db[...] = jnp.zeros_like(db)
     for s in (qs, dos, qns, dons):
         s[...] = jnp.zeros_like(s)
-    bwd_queries(pairs, do_ref, ot, qn, qt, qs, dos, qns, dons, dl)
+    for i in range(4):
+        bwd_query(pairs, i, do_ref, ot, qn, qt, qs, dos, qns, dons, dl)
     for r in list(range(1, nz)) + [0]:
         dk[...] = jnp.zeros_like(dk)
         dv[...] = jnp.zeros_like(dv)
@@ -662,50 +659,68 @@
     bv = sms[c, 1:2, :]
     bkvt[...] = jnp.broadcast_to(bv, (8, half)).T[:, 0:1]
     own_x.wait()
-    for s in range(2):
-        core[0, s].wait_recv()
+    core[0, 0].wait_recv()
+    core[0, 1].wait_recv()
     project_queries(pairs, xs, ws.at[:, 0:256], sms.at[c, 0:1], qn, qt, qs)
     copy(qn, qn_o)
     copy(qt, qt_o)
 
-    def chunk(r):
-        project_chunk(pairs, r, xs, ws.at[:, 256:768], wkvt, sms.at[c, 1:2], bkvt, K, V, KT, VT)
+    def bring(r, s):
+        if r:
+            core[r, s].wait_recv()
+        project_chunk(pairs, r, xs, ws.at[:, 256:768], wkvt, sms.at[c, 1:2], bkvt, K, V, KT, VT, 2 * s, 2 * s + 2)
         for a, b in ((xs, xall), (K, K_o), (V, V_o), (KT, KT_o)):
-            copy(a.at[r], b.at[r])
-
-    def attend(r, start, stop):
-        def step(i, _):
-            fwd_step(pairs, r, i, r == 0, K, VT, qs, m_s, l_s, acc, d_s, sb, pb)
+            if s:
+                copy(a.at[r], b.at[r])
+
+    def attend(r, js, last=False):
+        def step(n, _):
+            i = lax.rem(n + 2, 4) if last else n
+            fwd_step(pairs, r, i, r == 0, K, VT, qs, m_s, l_s, acc, d_s, sb, pb, js)
+            if last:
+                fwd_finish(pairs, i, m_s, l_s, acc, lse, ot, o_s)
+                for p in outs:
+                    pl.when(i == p)(outs[p].start)
             return 0
-        lax.fori_loop(start, stop, step, 0)
-
-    chunk(0)
+        lax.fori_loop(0, 4, step, 0)
+
+    def half_chunk(r, s, last=False):
+        bring(r, s)
+        attend(r, (2 * s, 2 * s + 1), last)
+
+    cols = pl.ds(pl.multiple_of(c * half, half), half)
+    outs = {p: w.make(o_s.at[p], att.at[y, :, cols], to[k]) for p, k in ((2, "y"), (3, "yc"), (1, "core"))}
+    bring(0, 0)
+    bring(0, 1)
     pump(1, 1)
-    attend(0, 0, 2)
-    attend(0, 2, 4)
-    for r in range(1, nz):
-        if r + 1 < nz:
+    attend(0, (0, 1, 2, 3))
+    for k, (a, b) in enumerate(((wos, wo), (wus, wu), (wds, wd))):
+        local[4 + k].wait()
+        n = a.shape[0] // 2
+        copy(a.at[rows_of(wi * n, n)], b.at[rows_of(wi * n, n)])
+    pump(2, 0)
+    for r in range(1, nz - 1):
+        half_chunk(r, 0)
+        if r > 1:
             pump(r + 1, 0)
-        for s in range(2):
-            core[r, s].wait_recv()
-        chunk(r)
-        attend(r, 0, 2)
-        if r + 1 < nz:
+        half_chunk(r, 1)
+        if r < nz - 2:
             pump(r + 1, 1)
-            share(r - 1)
-        attend(r, 2, 4)
-    fwd_finish(pairs, m_s, l_s, acc, lse, ot, o_s)
-    cols = pl.ds(pl.multiple_of(c * half, half), half)
-    outs = [w.go(o_s.at[p], att.at[y, :, cols], to[k]) for p, k in ((1, "core"), (2, "y"), (3, "yc"))]
+    half_chunk(nz - 1, 0)
+    pump(nz - 1, 1)
+    half_chunk(nz - 1, 1, True)
     copy(o_s.at[0], att.at[y, :, cols])
     copy(ot, ot_o)
     copy(lse, lse_o)
-    share(2)
+    for k, (a, b) in enumerate(((wos, wo), (wus, wu), (wds, wd))):
+        share(k)
+        copy(a.at[sent[k][2]], b.at[sent[k][2]])
     for k, (a, b) in enumerate(((wos, wo), (wus, wu), (wds, wd))):
         shared[k].wait_recv()
-        local[4 + k].wait()
-        copy(a, b)
-    for cp in outs:
+        n = a.shape[0] // 2
+        where = rows_of((1 - wi) * n + (1 - c) * (n // 2), n // 2)
+        copy(a.at[where], b.at[where])
+    for cp in outs.values():
         cp.wait_recv()
     w.drain()
     for cp in local[7:]:
@@ -761,7 +776,9 @@
     first_in = [copy(do_ref.at[y, :, cols], do.at[0])] + [copy(a, b) for a, b in ((qn_h, qn), (qt_h, qt), (ot_h, ot), (lse_h, lse))]
     kv_in = {}
     for r in list(range(1, nz)) + [0]:
-        kv_in[r] = [copy(a.at[r], b.at[r]) for a, b in ((K_h, K), (V_h, V), (KT_h, KT), (x_hbm, xs))]
+        kv_in[r] = [copy(a.at[r], b.at[r]) for a, b in ((K_h, K), (V_h, V), (KT_h, KT))]
+    for r in kv_in:
+        kv_in[r].append(copy(x_hbm.at[r], xs.at[r]))
     w_in = copy(w_hbm, wqkv)
 
     n = range(5)
@@ -913,13 +930,10 @@
     x_send(0)
     for cp in first_in:
         cp.wait()
-    for cp in dos_in:
-        cp.wait_recv()
-    bwd_queries(pairs, do, ot, qn, qt, qs, dos, qns, dons, dl)
     for r in kv_in:
-        for cp in kv_in[r]:
+        for cp in kv_in[r][:3]:
             cp.wait()
-    w_in.wait()
+    dos_in[2].wait_recv()
     hooks = plan(dict(x=x_send, y=y_send, za=z_a, zb=z_b, zc=z_c, zd=z_d, ys=y_share, cs=c_share, fold=fold, hop=hop, z=z_send, zs=z_share, vec=vec_send))
     hook = lambda *k: hooks[k]() if k in hooks else None
     hook("pre")
@@ -928,12 +942,20 @@
         dv[...] = jnp.zeros_like(dv)
         for n, js in enumerate(((2, 3), (0, 1)) if r == 1 else ((0, 1, 2, 3),)):
             def step(i, _):
+                if r == 1 and n == 0:
+                    for k in range(2):
+                        pl.when(i == 2)(dos_in[k].wait_recv)
+                    bwd_query(pairs, i, do, ot, qn, qt, qs, dos, qns, dons, dl)
                 bwd_step(pairs, r, i, r == 0, r == 1 and n == 0, K, V, KT, qs, dos, qns, dons, lse, dl, dk, dv, dq, d_s, gb, js)
                 for k in range(4):
                     if (r, n, k) in hooks:
                         pl.when(i == k)(hooks[r, n, k])
                 return 0
             lax.fori_loop(0, 4, step, 0)
+            if r == 1 and n == 0:
+                for q in kv_in:
+                    kv_in[q][3].wait()
+                w_in.wait()
             if r == 0:
                 bwd_query_out(pairs, xs, wqkv, dq, dxq, dw, db)
                 hook(0, 0, "q")

time: 180 us -> 175 us (0.972); the launches traced: 180 us -> 173 us
  Pallas kernels: 179 us -> 172 us
    pallas_call x1, Pallas kernels: 99.5 us -> 94.1 us  [back(): pl.pallas_call(functools.partial(back_kernel, nz), out_shape=(sds((2, 256...]
where the time goes in v1:
time: 175 us; the launch traced here: 173 us
  Pallas kernels  172 us (98%)
    pallas_call x1, Pallas kernels, back(): pl.pallas_call(functools.partial(back_kernel, nz), out_shape=(sds((2, 256...  94.1 us
    pallas_call x1, Pallas kernels, front(): pl.pallas_call(functools.partial(front_kernel, nz), out_shape=tuple(outs)...  58.2 us
    pallas_call x1, Pallas kernels, dense(): pl.pallas_call(dense_kernel, out_shape=(jax.ShapeDtypeStruct((tok, dim),...  14.7 us
    pallas_call x1, Pallas kernels, last(): pl.pallas_call(functools.partial(last_kernel, nu), out_shape=outs, in_spe...  5.32 us

profile of v1, /device:TPU:0, one launch (start us, length us, event | category | flops | bytes accessed | tf_op | source)
XLA Modules:
  0.0 173.1 jit_solution(17712271188007863567)
XLA Ops:
  0.7 58.2 %front.1 = (bf16[2,256,512]{2,1,0:T(8,128)(2,1)}, bf16[512,512]{1,0:T(8,128)(2,1)}, bf16[512,2048]{1,0:T(8,128)(2,1)}, bf16[2048,512]{1,0:T(8,128)(2,1)}, f32[2,...) custom-call(s32[2,32]{1,0:T(2,128)} %order_ref.3, ...), custom_call_target="tpu_custom_call" | custom-call | tf_op jit(solution)/shard_map/front/pallas_call | solution.py:743
  58.9 14.7 %dense.1 = (bf16[512,512]{1,0:T(8,128)(2,1)}, f32[512,512]{1,0:T(8,128)}, bf16[512,512]{1,0:T(8,128)(2,1)}, bf16[2,2304,512]{2,1,0:T(8,128)(2,1)}, f32[16,512]{1,0:T(8,128)}) custom-call(bf16[512,512]{1,0:T(8,128)(2,1)} %bitcast.8, bf16[512,512]{1,0:T(8,128)(2,1)} %bitcast.10, bf16[512,512]{1,0:T(8,128)(2,1)} %bitcast.12, ...), custom_call_target="tpu_custom_call" | custom-call | tf_op jit(solution)/shard_map/dense/pallas_call | solution.py:417
  73.5 94.1 %back.1 = (bf16[2,256,512]{2,1,0:T(8,128)(2,1)}, bf16[3,768,512]{2,1,0:T(8,128)(2,1)}, bf16[2,768,256]{2,1,0:T(8,128)(2,1)}, f32[24,512]{1,0:T(8,128)}) custom-call(s32[2,32]{1,0:T(2,128)} %order_ref.3, f32[16,512]{1,0:T(8,128)} %get-tuple-element.62.gv_ref, bf16[2,256,512]{2,1,0:T(8,128)(2,1)} %bitcast.11, ...), custom_call_target="tpu_custom_call" | custom-call | tf_op jit(solution)/shard_map/back/pallas_call | solution.py:1025
  167.6 5.3 %last.1 = (bf16[2,256,512]{2,1,0:T(8,128)(2,1)}, f32[256,512]{1,0:T(8,128)}, f32[256]{0:T(256)}, f32[256,512]{1,0:T(8,128)}, f32[256,512]{1,0:T(8,128)}, /*index...) custom-call(bf16[2304,512]{1,0:T(8,128)(2,1)} %bitcast.7, ...), custom_call_target="tpu_custom_call" | custom-call | tf_op jit(solution)/shard_map/last/pallas_call | solution.py:1066

commit v2 on v1

--- a/solution.py
+++ b/solution.py
@@ -227,14 +227,14 @@
         g = p * (dot(v, dos[i, u]) - dl[i, u])
         return p.astype(bf16), g.astype(bf16)
 
-    p, g = pieces(K[r, 0, part, :], V[r, 0, part, :], 1, None)
+    p, g = pieces(K[r][0, part, :], V[r][0, part, :], 1, None)
     dv[0, part, :] += dot(p, dons[i, 1])
     dk[0, part, :] += dot(g, qns[i, 1])
-    q_hi = by_pair(KT[r, 0, :, part], g)
+    q_hi = by_pair(KT[r][0, :, part], g)
     for j in js:
         u = jnp.where(pick[j], 0, 1)
         rows = slice(j * BLOCK, (j + 1) * BLOCK)
-        p, g = pieces(K[r, u, rows, :], V[r, u, rows, :], u, jnp.where(i == j, 0, 2 * BLOCK) if own else None)
+        p, g = pieces(K[r][u, rows, :], V[r][u, rows, :], u, jnp.where(i == j, 0, 2 * BLOCK) if own else None)
         gv, gk = dot(p, dons[i, u]), dot(g, qns[i, u])
         dv[0, rows, :] += jnp.where(pick[j], gv, 0.0)
         dv[1, rows, :] += jnp.where(pick[j], 0.0, gv)
@@ -243,14 +243,14 @@
         zero = jnp.zeros_like(g)
         gb[0, rows, :] = jnp.where(pick[j], g, zero)
         gb[1, rows, :] = jnp.where(pick[j], zero, g)
-    q_hi = q_hi + by_pair(KT[r, 1, :, part], gb[1, part, :])
-    q_lo = by_pair(KT[r, 0, :, part], gb[0, part, :])
+    q_hi = q_hi + by_pair(KT[r][1, :, part], gb[1, part, :])
+    q_lo = by_pair(KT[r][0, :, part], gb[0, part, :])
     if own:
         rows = pl.ds(pl.multiple_of(i * BLOCK, BLOCK), BLOCK)
-        p, g = pieces(K[r, 0, rows, :], V[r, 0, rows, :], 0, 0)
+        p, g = pieces(K[r][0, rows, :], V[r][0, rows, :], 0, 0)
         dv[0, rows, :] += dot(p, dons[i, 0])
         dk[0, rows, :] += dot(g, qns[i, 0])
-        q_lo = q_lo + by_pair(KT[r, 0, :, rows], g)
+        q_lo = q_lo + by_pair(KT[r][0, :, rows], g)
     if first:
         dq[i, 1], dq[i, 0] = q_hi, q_lo
     else:
@@ -301,6 +301,7 @@
 
 def bwd_local(nz, blk_ref, x_ref, wqkv_ref, K, V, KT, qn, qt, ot, lse, do_ref, dx, gq, db, qs, dos, qns, dons, dl, dk, dv, dq, d_s, gb, dxq, dw, gp):
     pairs = Pairs(nz * 8, lambda n: blk_ref[2 * n])
+    kv = [[a.at[r] for r in range(nz)] for a in (K, V, KT)]
     diagonal(d_s)
     dw[...] = jnp.zeros_like(dw)
     db[...] = jnp.zeros_like(db)
@@ -312,7 +313,7 @@
         dk[...] = jnp.zeros_like(dk)
         dv[...] = jnp.zeros_like(dv)
         def step(i, _):
-            bwd_step(pairs, r, i, r == 0, r == 1, K, V, KT, qs, dos, qns, dons, lse, dl, dk, dv, dq, d_s, gb)
+            bwd_step(pairs, r, i, r == 0, r == 1, *kv, qs, dos, qns, dons, lse, dl, dk, dv, dq, d_s, gb)
             return 0
         lax.fori_loop(0, 4, step, 0)
         if r == 0:
@@ -645,7 +646,7 @@
     def share(k):
         cp, full, where = sent[k]
         cp.wait_recv()
-        shared.append(w.go(full.at[where], full.at[where], to["core"]))
+        shared.append(w.go(full.at[where], (wo, wu, wd)[k].at[where], to["core"]))
 
     pump(1, 0)
     for cp in own_w:
@@ -715,11 +716,8 @@
     for k, (a, b) in enumerate(((wos, wo), (wus, wu), (wds, wd))):
         share(k)
         copy(a.at[sent[k][2]], b.at[sent[k][2]])
-    for k, (a, b) in enumerate(((wos, wo), (wus, wu), (wds, wd))):
-        shared[k].wait_recv()
-        n = a.shape[0] // 2
-        where = rows_of((1 - wi) * n + (1 - c) * (n // 2), n // 2)
-        copy(a.at[where], b.at[where])
+    for cp in shared:
+        cp.wait_recv()
     for cp in outs.values():
         cp.wait_recv()
     w.drain()
@@ -776,7 +774,7 @@
     first_in = [copy(do_ref.at[y, :, cols], do.at[0])] + [copy(a, b) for a, b in ((qn_h, qn), (qt_h, qt), (ot_h, ot), (lse_h, lse))]
     kv_in = {}
     for r in list(range(1, nz)) + [0]:
-        kv_in[r] = [copy(a.at[r], b.at[r]) for a, b in ((K_h, K), (V_h, V), (KT_h, KT))]
+        kv_in[r] = [copy(a.at[r], b[r]) for a, b in ((K_h, K), (V_h, V), (KT_h, KT))]
     for r in kv_in:
         kv_in[r].append(copy(x_hbm.at[r], xs.at[r]))
     w_in = copy(w_hbm, wqkv)
@@ -792,6 +790,7 @@
     Y_sum = [ys_.at[s] for s in range(3)] + [ysq.at[s] for s in range(2)]
     Z_in = [zrq.at[s] for s in range(2)]
     out = [gsum.at[s] for s in range(3)] + [gqsum.at[s] for s in range(2)]
+    done = [go.at[s] for s in range(3)] + [gqo.at[s] for s in range(2)]
     start_c, start_y = c * 384, c * 384 + y * 192
     at_c, at_y = rows_of(start_c, 384), rows_of(start_y, 192)
     pos = odd * 2 + far
@@ -804,7 +803,7 @@
         got["x", s] = w.make(cs.at[s, 1 - wi] if s < 3 else gq.at[1 - wi, pl.ds((s - 3) * 384, 384)], X_in[s], to["x"])
         got["y", s] = w.make(X_sum[s].at[theirs], Y_in[s], to["y"])
         got["ys", s] = w.make(out[s].at[at_y], out[s].at[at_y], to["y"])
-        got["cs", s] = w.make(out[s].at[at_c], out[s].at[at_c], to["core"])
+        got["cs", s] = w.make(out[s].at[at_c], done[s].at[at_c], to["core"])
         if s < 3:
             got["za", s] = w.make(ys_.at[s, rows_of((1 - odd) * 96, 96)], za.at[s], zp)
             got["zb", s] = w.make(zs.at[s, rows_of((1 - far) * 48, 48)], zb.at[s], zq)
@@ -874,6 +873,7 @@
     def c_share(s):
         got["ys", s].wait_recv()
         got["cs", s].start()
+        copy(out[s].at[at_c], done[s].at[at_c])
 
     for r in range(nz):
         for h in range(2):
@@ -881,7 +881,7 @@
             got["d", r, h] = w.make(dx.at[r, pl.ds(h * 512 + hrow, hrow)], dx_core.at[r, h], to["core"])
             if r:
                 got["r", (r + 1) % nz, h] = w.make(dx.at[r, at], dx_in.at[(r + 1) % nz, h], to["up"])
-    got["dy"] = w.make(dx.at[0, pl.ds(512, hrow)], outdx.at[1], to["y"])
+    got["dy"] = w.make(dx.at[0, pl.ds(512, hrow)], dxo.at[1], to["y"])
 
     def give(r, h):
         got["d", r, h].start()
@@ -900,6 +900,8 @@
             got["r", (r + 1) % nz, h].start()
         elif h:
             got["dy"].start()
+        else:
+            copy(outdx.at[0], dxo.at[0])
 
     vec_to = [to["core"], to["y"], to["x"]] + [(zz * 4 + low, wi) for zz in (z + 1 - 2 * lax.rem(z, 2), z + 2 - 4 * (z // 2))]
 
@@ -930,9 +932,6 @@
     x_send(0)
     for cp in first_in:
         cp.wait()
-    for r in kv_in:
-        for cp in kv_in[r][:3]:
-            cp.wait()
     dos_in[2].wait_recv()
     hooks = plan(dict(x=x_send, y=y_send, za=z_a, zb=z_b, zc=z_c, zd=z_d, ys=y_share, cs=c_share, fold=fold, hop=hop, z=z_send, zs=z_share, vec=vec_send))
     hook = lambda *k: hooks[k]() if k in hooks else None
@@ -940,6 +939,8 @@
     for r in list(range(1, nz)) + [0]:
         dk[...] = jnp.zeros_like(dk)
         dv[...] = jnp.zeros_like(dv)
+        for cp in kv_in[r][:3]:
+            cp.wait()
         for n, js in enumerate(((2, 3), (0, 1)) if r == 1 else ((0, 1, 2, 3),)):
             def step(i, _):
                 if r == 1 and n == 0:
@@ -972,9 +973,7 @@
     hook("tail")
     for s in range(5):
         got["cs", s].wait_recv()
-        copy(gsum.at[s], go.at[s]) if s < 3 else copy(gqsum.at[s - 3], gqo.at[s - 3])
     got["dy"].wait_recv()
-    copy(outdx, dxo)
     w.drain()
     for cp in local[-6:]:
         cp.wait()
@@ -982,8 +981,8 @@
 
 PLAN = {
     (1, 0, "r"): (("x", 2),),
+    (1, 1, 1): (("fold", 1, 1),),
     (1, 1, 2): (("y", 0),),
-    (1, 1, "r"): (("fold", 1, 1),),
     (2, 0, 2): (("x", 1), ("fold", 1, 0), ("za", 0),),
     (2, 0, "r"): (("y", 2),),
     (3, 0, 2): (("zb", 0),),
@@ -1015,8 +1014,8 @@
     B = lambda *s: pltpu.VMEM(s, bf16)
     F = lambda *s: pltpu.VMEM(s, f32)
     ins = (x_all, wqkv, k, v, kt, qn, qt, ot, lse)
-    scratch = [pltpu.VMEM(a.shape, a.dtype) for a in ins] + [B(4, 256, 256)] + bwd_scratch()
-    scratch += [B(nz, 1024, 512), B(1024, 512), B(2, 768, 256), F(8, 256), B(2, 256, 512)]
+    scratch = [[pltpu.VMEM(a.shape[1:], a.dtype)] * nz if any(a is b for b in (k, v, kt)) else pltpu.VMEM(a.shape, a.dtype) for a in ins] + [B(4, 256, 256)] + bwd_scratch()
+    scratch += [B(nz, 1024, 512), B(1024, 512), B(2, 768, 256), F(8, 256), B(1, 256, 512)]
     scratch += [B(nz, 2, 256, 512), B(nz, 2, 256, 512), B(3, 2, 384, 512), B(3, 2, 384, 512), B(3, 384, 512), B(3, 384, 512), B(3, 192, 512), B(3, 192, 512),
                 B(3, 96, 512), B(3, 96, 512), B(3, 48, 512), B(2, 384, 256), B(2, 384, 256), B(2, 192, 256), B(2, 192, 256), B(2, nz - 1, 48, 256),
                 B(3, 768, 512), B(2, 768, 256),

time: 175 us -> 173 us (0.989)
  no operation moved by 1% of the time
where the time goes in v2:
time: 173 us
  Pallas kernels  172 us (99%)
    pallas_call x1, Pallas kernels, back(): pl.pallas_call(functools.partial(back_kernel, nz), out_shape=(sds((2, 256...  93.5 us
    pallas_call x1, Pallas kernels, front(): pl.pallas_call(functools.partial(front_kernel, nz), out_shape=tuple(outs)...  58.2 us
    pallas_call x1, Pallas kernels, dense(): pl.pallas_call(dense_kernel, out_shape=(jax.ShapeDtypeStruct((tok, dim),...  14.7 us
    pallas_call x1, Pallas kernels, last(): pl.pallas_call(functools.partial(last_kernel, nu), out_shape=outs, in_spe...  5.32 us

profile of v2, /device:TPU:0, one launch (start us, length us, event | category | flops | bytes accessed | tf_op | source)
XLA Modules:
  0.0 172.5 jit_solution(9008515739077033908)
XLA Ops:
  0.7 58.2 %front.1 = (bf16[2,256,512]{2,1,0:T(8,128)(2,1)}, bf16[512,512]{1,0:T(8,128)(2,1)}, bf16[512,2048]{1,0:T(8,128)(2,1)}, bf16[2048,512]{1,0:T(8,128)(2,1)}, f32[2,...) custom-call(s32[2,32]{1,0:T(2,128)} %order_ref.3, ...), custom_call_target="tpu_custom_call" | custom-call | tf_op jit(solution)/shard_map/front/pallas_call | solution.py:741
  58.8 14.7 %dense.1 = (bf16[512,512]{1,0:T(8,128)(2,1)}, f32[512,512]{1,0:T(8,128)}, bf16[512,512]{1,0:T(8,128)(2,1)}, bf16[2,2304,512]{2,1,0:T(8,128)(2,1)}, f32[16,512]{1,0:T(8,128)}) custom-call(bf16[512,512]{1,0:T(8,128)(2,1)} %bitcast.8, bf16[512,512]{1,0:T(8,128)(2,1)} %bitcast.10, bf16[512,512]{1,0:T(8,128)(2,1)} %bitcast.12, ...), custom_call_target="tpu_custom_call" | custom-call | tf_op jit(solution)/shard_map/dense/pallas_call | solution.py:418
  73.5 93.5 %back.1 = (bf16[2,256,512]{2,1,0:T(8,128)(2,1)}, bf16[3,768,512]{2,1,0:T(8,128)(2,1)}, bf16[2,768,256]{2,1,0:T(8,128)(2,1)}, f32[24,512]{1,0:T(8,128)}) custom-call(s32[2,32]{1,0:T(2,128)} %order_ref.3, f32[16,512]{1,0:T(8,128)} %get-tuple-element.62.gv_ref, bf16[2,256,512]{2,1,0:T(8,128)(2,1)} %bitcast.11, ...), custom_call_target="tpu_custom_call" | custom-call | tf_op jit(solution)/shard_map/back/pallas_call | solution.py:1024
  167.0 5.3 %last.1 = (bf16[2,256,512]{2,1,0:T(8,128)(2,1)}, f32[256,512]{1,0:T(8,128)}, f32[256]{0:T(256)}, f32[256,512]{1,0:T(8,128)}, f32[256,512]{1,0:T(8,128)}, /*index...) custom-call(bf16[2304,512]{1,0:T(8,128)(2,1)} %bitcast.7, ...), custom_call_target="tpu_custom_call" | custom-call | tf_op jit(solution)/shard_map/last/pallas_call | solution.py:1065

commit v3 on v2

--- a/solution.py
+++ b/solution.py
@@ -988,9 +988,10 @@
     (3, 0, 2): (("zb", 0),),
     (3, 0, 3): (("za", 2), ("fold", 2, 0), ("y", 1),),
     (3, 0, "r"): (("zc", 0), ("hop", 2, 0),),
+    (0, 0, 0): (("fold", 2, 1), ("hop", 2, 1),),
     (0, 0, 2): (("za", 1),),
-    (0, 0, "q"): (("zb", 2), ("zd", 0), ("fold", 2, 1),),
-    (0, 0, "w"): (("hop", 2, 1), ("zc", 2), ("vec", 0), ("zb", 1), ("fold", 3, 1), ("fold", 3, 0), ("y", 3), ("x", 4), ("zd", 2), ("zc", 1), ("ys",
+    (0, 0, "q"): (("zb", 2), ("zd", 0), ),
+    (0, 0, "w"): (("zc", 2), ("vec", 0), ("zb", 1), ("fold", 3, 1), ("fold", 3, 0), ("y", 3), ("x", 4), ("zd", 2), ("zc", 1), ("ys",
         0), ("z", 3), ("y", 4),),
     (0, 0, "r"): (("zd", 1), ("fold", 0, 1), ("hop", 3, 1), ("zs", 3), ("ys", 2), ("z", 4),),
     "tail": (("fold", 0, 0), ("vec", 1), ("ys", 1), ("ys", 3), ("vec", 2), ("cs", 0), ("zs", 4), ("vec", 3), ("hop", 3, 0), ("cs", 2), ("hop", 0, 1),

time: 173 us -> 172 us (level)
  no operation moved by 1% of the time
where the time goes in v3:
time: 172 us
  Pallas kernels  171 us (99%)
    pallas_call x1, Pallas kernels, back(): pl.pallas_call(functools.partial(back_kernel, nz), out_shape=(sds((2, 256...  92.6 us
    pallas_call x1, Pallas kernels, front(): pl.pallas_call(functools.partial(front_kernel, nz), out_shape=tuple(outs)...  58.2 us
    pallas_call x1, Pallas kernels, dense(): pl.pallas_call(dense_kernel, out_shape=(jax.ShapeDtypeStruct((tok, dim),...  14.7 us
    pallas_call x1, Pallas kernels, last(): pl.pallas_call(functools.partial(last_kernel, nu), out_shape=outs, in_spe...  5.32 us

profile of v3, /device:TPU:0, one launch (start us, length us, event | category | flops | bytes accessed | tf_op | source)
XLA Modules:
  0.0 171.6 jit_solution(11791249313417524160)
XLA Ops:
  0.7 58.2 %front.1 = (bf16[2,256,512]{2,1,0:T(8,128)(2,1)}, bf16[512,512]{1,0:T(8,128)(2,1)}, bf16[512,2048]{1,0:T(8,128)(2,1)}, bf16[2048,512]{1,0:T(8,128)(2,1)}, f32[2,...) custom-call(s32[2,32]{1,0:T(2,128)} %order_ref.3, ...), custom_call_target="tpu_custom_call" | custom-call | tf_op jit(solution)/shard_map/front/pallas_call | solution.py:741
  58.8 14.7 %dense.1 = (bf16[512,512]{1,0:T(8,128)(2,1)}, f32[512,512]{1,0:T(8,128)}, bf16[512,512]{1,0:T(8,128)(2,1)}, bf16[2,2304,512]{2,1,0:T(8,128)(2,1)}, f32[16,512]{1,0:T(8,128)}) custom-call(bf16[512,512]{1,0:T(8,128)(2,1)} %bitcast.8, bf16[512,512]{1,0:T(8,128)(2,1)} %bitcast.10, bf16[512,512]{1,0:T(8,128)(2,1)} %bitcast.12, ...), custom_call_target="tpu_custom_call" | custom-call | tf_op jit(solution)/shard_map/dense/pallas_call | solution.py:418
  73.5 92.6 %back.1 = (bf16[2,256,512]{2,1,0:T(8,128)(2,1)}, bf16[3,768,512]{2,1,0:T(8,128)(2,1)}, bf16[2,768,256]{2,1,0:T(8,128)(2,1)}, f32[24,512]{1,0:T(8,128)}) custom-call(s32[2,32]{1,0:T(2,128)} %order_ref.3, f32[16,512]{1,0:T(8,128)} %get-tuple-element.62.gv_ref, bf16[2,256,512]{2,1,0:T(8,128)(2,1)} %bitcast.11, ...), custom_call_target="tpu_custom_call" | custom-call | tf_op jit(solution)/shard_map/back/pallas_call | solution.py:1025
  166.1 5.3 %last.1 = (bf16[2,256,512]{2,1,0:T(8,128)(2,1)}, f32[256,512]{1,0:T(8,128)}, f32[256]{0:T(256)}, f32[256,512]{1,0:T(8,128)}, f32[256,512]{1,0:T(8,128)}, /*index...) custom-call(bf16[2304,512]{1,0:T(8,128)(2,1)} %bitcast.7, ...), custom_call_target="tpu_custom_call" | custom-call | tf_op jit(solution)/shard_map/last/pallas_call | solution.py:1066

commit v4 on v3

--- a/solution.py
+++ b/solution.py
@@ -983,7 +983,8 @@
     (1, 0, "r"): (("x", 2),),
     (1, 1, 1): (("fold", 1, 1),),
     (1, 1, 2): (("y", 0),),
-    (2, 0, 2): (("x", 1), ("fold", 1, 0), ("za", 0),),
+    (2, 0, 1): (("fold", 1, 0),),
+    (2, 0, 2): (("x", 1), ("za", 0),),
     (2, 0, "r"): (("y", 2),),
     (3, 0, 2): (("zb", 0),),
     (3, 0, 3): (("za", 2), ("fold", 2, 0), ("y", 1),),

time: 172 us -> 173 us (level)
  no operation moved by 1% of the time
where the time goes in v4:
time: 173 us
  Pallas kernels  172 us (99%)
    pallas_call x1, Pallas kernels, back(): pl.pallas_call(functools.partial(back_kernel, nz), out_shape=(sds((2, 256...  94.2 us
    pallas_call x1, Pallas kernels, front(): pl.pallas_call(functools.partial(front_kernel, nz), out_shape=tuple(outs)...  58.2 us
    pallas_call x1, Pallas kernels, dense(): pl.pallas_call(dense_kernel, out_shape=(jax.ShapeDtypeStruct((tok, dim),...  14.7 us
    pallas_call x1, Pallas kernels, last(): pl.pallas_call(functools.partial(last_kernel, nu), out_shape=outs, in_spe...  5.32 us

profile of v4, /device:TPU:0, one launch (start us, length us, event | category | flops | bytes accessed | tf_op | source)
XLA Modules:
  0.0 173.2 jit_solution(11315150801114223915)
XLA Ops:
  0.7 58.2 %front.1 = (bf16[2,256,512]{2,1,0:T(8,128)(2,1)}, bf16[512,512]{1,0:T(8,128)(2,1)}, bf16[512,2048]{1,0:T(8,128)(2,1)}, bf16[2048,512]{1,0:T(8,128)(2,1)}, f32[2,...) custom-call(s32[2,32]{1,0:T(2,128)} %order_ref.3, ...), custom_call_target="tpu_custom_call" | custom-call | tf_op jit(solution)/shard_map/front/pallas_call | solution.py:741
  58.8 14.7 %dense.1 = (bf16[512,512]{1,0:T(8,128)(2,1)}, f32[512,512]{1,0:T(8,128)}, bf16[512,512]{1,0:T(8,128)(2,1)}, bf16[2,2304,512]{2,1,0:T(8,128)(2,1)}, f32[16,512]{1,0:T(8,128)}) custom-call(bf16[512,512]{1,0:T(8,128)(2,1)} %bitcast.8, bf16[512,512]{1,0:T(8,128)(2,1)} %bitcast.10, bf16[512,512]{1,0:T(8,128)(2,1)} %bitcast.12, ...), custom_call_target="tpu_custom_call" | custom-call | tf_op jit(solution)/shard_map/dense/pallas_call | solution.py:418
  73.5 94.2 %back.1 = (bf16[2,256,512]{2,1,0:T(8,128)(2,1)}, bf16[3,768,512]{2,1,0:T(8,128)(2,1)}, bf16[2,768,256]{2,1,0:T(8,128)(2,1)}, f32[24,512]{1,0:T(8,128)}) custom-call(s32[2,32]{1,0:T(2,128)} %order_ref.3, f32[16,512]{1,0:T(8,128)} %get-tuple-element.62.gv_ref, bf16[2,256,512]{2,1,0:T(8,128)(2,1)} %bitcast.11, ...), custom_call_target="tpu_custom_call" | custom-call | tf_op jit(solution)/shard_map/back/pallas_call | solution.py:1026
  167.8 5.3 %last.1 = (bf16[2,256,512]{2,1,0:T(8,128)(2,1)}, f32[256,512]{1,0:T(8,128)}, f32[256]{0:T(256)}, f32[256,512]{1,0:T(8,128)}, f32[256,512]{1,0:T(8,128)}, /*index...) custom-call(bf16[2304,512]{1,0:T(8,128)(2,1)} %bitcast.7, ...), custom_call_target="tpu_custom_call" | custom-call | tf_op jit(solution)/shard_map/last/pallas_call | solution.py:1067
